TPU v7x, 256 devices: a whole 4x4x8 slice. The times are simulated.
256 devices in a mesh: row: 8 (over x, core), col: 4 (over z_lo), tp: 8 (over y, z_hi).
Axes of the slice: x: 4, y: 4, z: 8 (z_hi: 2, z_lo: 4; z = z_hi * 4 + z_lo), core: 2. Of those that a mesh axis runs over, the one named last changes fastest.
Arguments:
- tokens: bfloat16 [16384, 1024], P(('row', 'col'), 'tp'), may hold values from -6 to 6
- norm_before: bfloat16 [2, 1024], replicated, may hold values from 0.099609375 to 1.8984375
- query_weight: bfloat16 [2, 1024, 1024], P(None, None, 'tp'), may hold values from -0.1875 to 0.1875
- key_weight: bfloat16 [2, 1024, 1024], P(None, None, 'tp'), may hold values from -8 to 8
- value_weight: bfloat16 [2, 1024, 1024], P(None, None, 'tp'), may hold values from -0.1875 to 0.1875
- output_weight: bfloat16 [2, 1024, 1024], P(None, 'tp'), may hold values from -0.375 to 0.375
- norm_after: bfloat16 [2, 1024], replicated, may hold values from 0.099609375 to 1.8984375
- gate_weight: bfloat16 [2, 1024, 4096], P(None, None, 'tp'), may hold values from -0.1875 to 0.1875
- up_weight: bfloat16 [2, 1024, 4096], P(None, None, 'tp'), may hold values from -0.1875 to 0.1875
- down_weight: bfloat16 [2, 4096, 1024], P(None, 'tp'), may hold values from -0.09375 to 0.09375
- block_image: int32 [128], replicated, may hold values from 0 to 7, never falling along the last dimension, each value on 1 to 29 neighbouring positions
- image_width: int32 [8], replicated, may hold values from 16 to 64
Outputs:
- encoded: float32 [16384, 1024], P(('row', 'col'), 'tp')
Inputs may be any that keep to these rules, and one draw needn't show every extreme that they name: `block_image`: image numbers never fall from block to block; each image fills 1 to 29 whole blocks of 128 patch slots, and one image fills exactly 29.
All inputs are finite; a program needn't handle non-finite values.
Results may differ from a plain program's by a relative error of at most 0.035.
The roundings to bfloat16 on the way count: a program that leaves them out, or rounds other values in their place, can miss the bound.
Values may be sent and summed in bfloat16 or wider, within the bound.
A program may use at most 64 MiB of HBM per device.

v0:
```python
import jax
import jax.numpy as jnp
from jax import lax
from jax.sharding import PartitionSpec as P

HEAD_DIM = 64
BLK = 128
SPAN = 32


epsilon = 1e-05
theta = 10000.0
masked = -1e30


def shifted(x, axis, by):
    size = lax.axis_size(axis)
    pairs = [(i, i + by) for i in range(size) if 0 <= i + by < size]
    return lax.ppermute(x, axis, pairs)


def in_blocks(x, dim, size):
    before, after = (x.shape[:dim], x.shape[dim + 1 :])
    return jnp.moveaxis(x.reshape(*before, size, -1, *after), dim, 0)


def summed_on_arrival(x, axis, dim):
    tiles = in_blocks(x, dim, lax.axis_size(axis))
    arrived = lax.all_to_all(tiles, axis, split_axis=0, concat_axis=0, tiled=True)
    return arrived.sum(axis=0)


def from_everyone(x, axis):
    size = lax.axis_size(axis)
    return lax.all_to_all(jnp.broadcast_to(x[None], (size, *x.shape)), axis, 0, 0, tiled=True)


def joined_along(tiles, dim):
    shape = list(tiles.shape[1:])
    shape[dim] *= tiles.shape[0]
    return jnp.moveaxis(tiles, 0, dim).reshape(shape)


def collect(x, axis, dim):
    tiles = from_everyone(x, axis)
    return joined_along(tiles, dim)


def block_tables(block_image, image_width):
    block_total = block_image.shape[0]
    images = jnp.arange(image_width.shape[0], dtype=jnp.int32)
    member = (block_image[:, None] == images[None, :]).astype(jnp.int32)
    count = jnp.sum(member, axis=0)
    start = jnp.sum((block_image[:, None] < images[None, :]).astype(jnp.int32), axis=0)
    slots = count * BLK
    filled = slots // image_width * image_width
    first = jnp.sum(member * start[None, :], axis=1)
    offset = (jnp.arange(block_total, dtype=jnp.int32) - first) * BLK
    return (
        block_image,
        offset,
        jnp.sum(member * image_width[None, :], axis=1),
        jnp.sum(member * filled[None, :], axis=1),
    )


def token_rows(tables, first_block, shard_blocks):
    image, offset, width, filled = [
        jnp.repeat(lax.dynamic_slice_in_dim(table, first_block, shard_blocks), BLK)
        for table in tables
    ]
    slot = offset + jnp.arange(shard_blocks * BLK, dtype=jnp.int32) % BLK
    return (image, slot // width, slot % width, slot < filled)


def key_tags(tables, device, devices, shard_blocks):
    inside = (device >= 0) & (device < devices)
    safe = jnp.clip(device, 0, devices - 1)
    image, patch_row, patch_column, live = token_rows(tables, safe * shard_blocks, shard_blocks)
    return jnp.where(inside & live, image, -1)


def rope_tables(patch_row, patch_column):
    half = HEAD_DIM // 2
    frequency = theta ** (-2.0 * jnp.arange(half, dtype=jnp.float32) / HEAD_DIM)
    angle = jnp.concatenate(
        [
            patch_row.astype(jnp.float32)[:, None] * frequency[None, 0::2],
            patch_column.astype(jnp.float32)[:, None] * frequency[None, 1::2],
        ],
        axis=1,
    )
    return (jnp.cos(angle), jnp.sin(angle))


def rotate(heads, cosine, sine):
    half = heads.shape[-1] // 2
    front = heads[..., :half]
    back = heads[..., half:]
    cosine = cosine[:, None, :]
    sine = sine[:, None, :]
    return jnp.concatenate([front * cosine - back * sine, back * cosine + front * sine], axis=-1)


def normalize(values, gain):
    scale = lax.rsqrt(jnp.mean(values * values, axis=-1, keepdims=True) + epsilon)
    return (values * scale * gain.astype(jnp.float32)).astype(jnp.bfloat16)


def attend(state, block, tags, query, query_image):
    best, total, summed = state
    rows = block.shape[0]
    heads = query.shape[1]
    depth = query.shape[2]
    keys = block[:, : heads * depth].reshape(rows, heads, depth)
    values = block[:, heads * depth :].reshape(rows, heads, depth)
    scores = jnp.einsum(
        "thd,uhd->thu", query, keys, preferred_element_type=jnp.float32
    ) * HEAD_DIM ** (-0.5)
    allowed = (query_image[:, None] == tags[None, :])[:, None, :]
    fresh = jnp.maximum(best, jnp.max(jnp.where(allowed, scores, masked), axis=-1))
    carry_scale = jnp.exp(best - fresh)
    raised = jnp.where(allowed, jnp.exp(scores - fresh[..., None]), 0.0)
    total = total * carry_scale + jnp.sum(raised, axis=-1)
    summed = summed * carry_scale[..., None] + jnp.einsum(
        "thu,uhd->thd", raised.astype(jnp.bfloat16), values, preferred_element_type=jnp.float32
    )
    return (fresh, total, summed)


def local(
    tokens,
    norm_before,
    query_weight,
    key_weight,
    value_weight,
    output_weight,
    norm_after,
    gate_weight,
    up_weight,
    down_weight,
    block_image,
    image_width,
):
    local_rows = tokens.shape[0]
    shard_blocks = local_rows // BLK
    reach = SPAN // shard_blocks - 1
    devices = lax.axis_size(("row", "col"))
    place = lax.axis_index(("row", "col"))
    tables = block_tables(block_image, image_width)
    own_image, patch_row, patch_column, own_live = token_rows(
        tables, place * shard_blocks, shard_blocks
    )
    own_tags = jnp.where(own_live, own_image, -1)
    cosine, sine = rope_tables(patch_row, patch_column)
    whole = lax.all_gather(tokens, "tp", axis=1, tiled=True).astype(jnp.float32)
    layer_input = tokens.astype(jnp.float32)
    layer_count = query_weight.shape[0]
    for layer in range(layer_count):
        normed = normalize(whole, norm_before[layer])
        query = jnp.dot(normed, query_weight[layer], preferred_element_type=jnp.float32)
        heads_here = query.shape[1] // HEAD_DIM
        query = rotate(query.reshape(local_rows, heads_here, HEAD_DIM), cosine, sine).astype(
            jnp.bfloat16
        )
        keys = jnp.dot(normed, key_weight[layer], preferred_element_type=jnp.float32)
        keys = rotate(keys.reshape(local_rows, heads_here, HEAD_DIM), cosine, sine).astype(
            jnp.bfloat16
        )
        values = jnp.dot(normed, value_weight[layer], preferred_element_type=jnp.float32).astype(
            jnp.bfloat16
        )
        pair = jnp.concatenate([keys.reshape(local_rows, heads_here * HEAD_DIM), values], axis=1)
        start_state = (
            jnp.full((local_rows, heads_here), masked, jnp.float32),
            jnp.zeros((local_rows, heads_here), jnp.float32),
            jnp.zeros((local_rows, heads_here, HEAD_DIM), jnp.float32),
        )
        state = attend(start_state, pair, own_tags, query, own_image)
        lower = pair[None]
        upper = pair[None]
        stride = 1
        while stride <= reach:
            lower = jnp.concatenate([lower, shifted(lower, ("row", "col"), stride)], axis=0)
            upper = jnp.concatenate([upper, shifted(upper, ("row", "col"), -stride)], axis=0)
            stride = stride * 2

        def visit(inner, items):
            below, above, distance = items
            tags = jnp.concatenate(
                [
                    key_tags(tables, place - distance, devices, shard_blocks),
                    key_tags(tables, place + distance, devices, shard_blocks),
                ]
            )
            return (
                attend(inner, jnp.concatenate([below, above], axis=0), tags, query, own_image),
                None,
            )

        state, unused = lax.scan(
            visit,
            state,
            (lower[1 : reach + 1], upper[1 : reach + 1], jnp.arange(1, reach + 1, dtype=jnp.int32)),
        )
        best, total, summed = state
        attended = (
            (summed / total[..., None])
            .reshape(local_rows, heads_here * HEAD_DIM)
            .astype(jnp.bfloat16)
        )
        mixed_part = jnp.dot(attended, output_weight[layer], preferred_element_type=jnp.float32)
        middle_own = layer_input + summed_on_arrival(mixed_part, "tp", 1)
        middle = collect(middle_own, "tp", 1)
        post = normalize(middle, norm_after[layer])
        gate = jnp.dot(post, gate_weight[layer], preferred_element_type=jnp.float32)
        up = jnp.dot(post, up_weight[layer], preferred_element_type=jnp.float32)
        hidden = (jax.nn.silu(gate) * up).astype(jnp.bfloat16)
        down_part = jnp.dot(hidden, down_weight[layer], preferred_element_type=jnp.float32)
        layer_input = middle_own + summed_on_arrival(down_part, "tp", 1)
        if layer + 1 < layer_count:
            whole = collect(layer_input, "tp", 1)
    return layer_input


def solution(mesh):
    placed = (
        P(("row", "col"), "tp"),
        P(),
        P(None, None, "tp"),
        P(None, None, "tp"),
        P(None, None, "tp"),
        P(None, "tp", None),
        P(),
        P(None, None, "tp"),
        P(None, None, "tp"),
        P(None, "tp", None),
        P(),
        P(),
    )
    return jax.shard_map(
        local, mesh=mesh, in_specs=placed, out_specs=P(("row", "col"), "tp"), check_vma=False
    )
```

profile of v0, /device:TPU:4, one launch (start us, length us, event | category | flops | bytes accessed | tf_op | source)
XLA Modules:
  0.0 730.4 jit_solution(4790978735277907035)
XLA Ops:
  17.5 57.0 %all-gather.2.cloned.1.call-done = bf16[512,1024]{1,0:T(8,128)(2,1)} async-done(((bf16[512,128]{1,0:T(8,128)(2,1)}), bf16[512,1024]{1,0:T(8,128)(2,1)}) %all-gather.2.cloned.1.call-update) | async-done | bytes 1048592 | tf_op jit(solution)/shard_map/all_gather | solution.py:156
  87.3 5.8 collective-permute-done
  101.1 31.8 %collective-permute-done.4 = bf16[2,512,256]{1,2,0:T(8,128)(2,1)S(1)} collective-permute-done((bf16[2,512,256]{1,2,0:T(8,128)(2,1)S(1)}, bf16[2,512,256]{1,2,0:T(8,128)(2,1)S(1)}, u32[]{:S(2)}, u32[]{:S(2)}) %collective-permute-start.4) | collective-permute-done | bytes 524320 | tf_op jit(solution)/shard_map/ppermute | solution.py:19
  133.0 9.3 %collective-permute-done.1 = bf16[2,512,256]{1,2,0:T(8,128)(2,1)S(1)} collective-permute-done((bf16[2,512,256]{1,2,0:T(8,128)(2,1)S(1)}, bf16[2,512,256]{1,2,0:T(8,128)(2,1)S(1)}, u32[]{:S(2)}, u32[]{:S(2)}) %collective-permute-start.1) | collective-permute-done | bytes 524320 | tf_op jit(solution)/shard_map/ppermute | solution.py:19
  150.4 7.2 collective-permute-done.5
  162.9 59.8 %while.34 = (s32[]{:T(128)}, f32[512,2]{0,1:T(2,128)S(1)}, f32[512,2]{0,1:T(2,128)S(1)}, f32[512,2,64]{0,2,1:T(8,128)}, s32[7]{0:T(128)S(1)}, /*index=5*/s32[]{:...) while((s32[]{:T(128)}, f32[512,2]{0,1:T(2,128)S(1)}, ...), condition=%wide.region_11.12_spmd.clone, body=%wide.region_8.11_spmd.clone.sunk | while | flops 281687040 | bytes 20140812 | solution.py:201
  224.8 55.4 %all_to_all.35 = f32[8,512,128]{2,1,0:T(8,128)S(1)} all-to-all(f32[8,512,128]{2,1,0:T(8,128)S(1)} %convolution_bitcast_fusion.3), channel_id=1, replica_groups=mesh['row'=8,'col'=4,'tp'=8] {'tp'}, dimensions={0} | all-to-all | bytes 4194304 | tf_op jit(solution)/shard_map/all_to_all | solution.py:29
  282.9 5.1 all-to-all-start.1
  293.0 35.5 %all-to-all-done.1 = f32[8,512,128]{1,2,0:T(8,128)S(1)} async-done(((f32[8,512,128]{1,2,0:T(8,128)}), f32[8,512,128]{1,2,0:T(8,128)S(1)}, u32[]{:S(2)}, u32[]{:S(2)}) %all-to-all-start.1) | async-done | bytes 2097184 | tf_op jit(solution)/shard_map/all_to_all | solution.py:35
  331.9 4.3 convolution_bitcast_fusion.1
  336.2 41.9 %all_to_all.36 = f32[8,512,128]{2,1,0:T(8,128)S(1)} all-to-all(f32[8,512,128]{2,1,0:T(8,128)} %convolution_bitcast_fusion.1), channel_id=1, replica_groups=mesh['row'=8,'col'=4,'tp'=8] {'tp'}, dimensions={0} | all-to-all | bytes 4194304 | tf_op jit(solution)/shard_map/all_to_all | solution.py:29
  386.9 36.2 %all-to-all-done.3 = f32[8,512,128]{2,1,0:T(8,128)S(1)} async-done(((f32[8,512,128]{2,1,0:T(8,128)}), f32[8,512,128]{2,1,0:T(8,128)S(1)}, u32[]{:S(2)}, u32[]{:S(2)}) %all-to-all-start.3) | async-done | bytes 2097184 | tf_op jit(solution)/shard_map/all_to_all | solution.py:35
  429.2 8.1 %collective-permute-start.9 = (bf16[1,512,256]{1,2,0:T(8,128)(2,1)S(1)}, bf16[1,512,256]{1,2,0:T(8,128)(2,1)S(1)}, u32[]{:S(2)}, u32[]{:S(2)}) collective-permute-start(bf16[1,512,256]{1,2,0:T(8,128)(2,1)S(1)} %maximum_bitcast_fusion.1), channel_id=1, source_target_pairs={{8,0},{16,8},{24,16},{32,24},{40,32},{48,40},{56,48},{64,56},{72,6... | collective-permute-start | bytes 786440 | tf_op jit(solution)/shard_map/ppermute | solution.py:19
  443.6 6.8 collective-permute-done.6
  452.3 4.8 collective-permute-start.7
  459.1 30.3 %collective-permute-done.10 = bf16[2,512,256]{1,2,0:T(8,128)(2,1)S(1)} collective-permute-done((bf16[2,512,256]{1,2,0:T(8,128)(2,1)S(1)}, bf16[2,512,256]{1,2,0:T(8,128)(2,1)S(1)}, u32[]{:S(2)}, u32[]{:S(2)}) %collective-permute-start.10) | collective-permute-done | bytes 524320 | tf_op jit(solution)/shard_map/ppermute | solution.py:19
  489.4 7.8 %collective-permute-done.7 = bf16[2,512,256]{1,2,0:T(8,128)(2,1)S(1)} collective-permute-done((bf16[2,512,256]{1,2,0:T(8,128)(2,1)S(1)}, bf16[2,512,256]{1,2,0:T(8,128)(2,1)S(1)}, u32[]{:S(2)}, u32[]{:S(2)}) %collective-permute-start.7) | collective-permute-done | bytes 524320 | tf_op jit(solution)/shard_map/ppermute | solution.py:19
  505.4 6.3 collective-permute-done.11
  517.0 53.1 %while.35 = (s32[]{:T(128)}, f32[512,2]{0,1:T(2,128)S(1)}, f32[512,2]{0,1:T(2,128)S(1)}, f32[512,2,64]{0,2,1:T(8,128)}, s32[7]{0:T(128)S(1)}, /*index=5*/s32[]{:...) while((s32[]{:T(128)}, f32[512,2]{0,1:T(2,128)S(1)}, ...), condition=%wide.region_21.22_spmd.clone, body=%wide.region_18.21_spmd.clone.sunk | while | flops 281687040 | bytes 20665128 | solution.py:201
  572.4 54.5 %all_to_all.37 = f32[8,512,128]{2,1,0:T(8,128)S(1)} all-to-all(f32[8,512,128]{2,1,0:T(8,128)S(1)} %convolution_bitcast_fusion.2), channel_id=1, replica_groups=mesh['row'=8,'col'=4,'tp'=8] {'tp'}, dimensions={0} | all-to-all | bytes 4194304 | tf_op jit(solution)/shard_map/all_to_all | solution.py:29
  630.5 6.6 all-to-all-start.5
  638.4 37.7 %all-to-all-done.5 = f32[8,512,128]{1,2,0:T(8,128)S(1)} async-done(((f32[8,512,128]{1,2,0:T(8,128)}), f32[8,512,128]{1,2,0:T(8,128)S(1)}, u32[]{:S(2)}, u32[]{:S(2)}) %all-to-all-start.5) | async-done | bytes 2097184 | tf_op jit(solution)/shard_map/all_to_all | solution.py:35
  679.2 4.0 convolution_bitcast_fusion
  683.2 38.7 %all_to_all.38 = f32[8,512,128]{2,1,0:T(8,128)S(1)} all-to-all(f32[8,512,128]{2,1,0:T(8,128)} %convolution_bitcast_fusion), channel_id=1, replica_groups=mesh['row'=8,'col'=4,'tp'=8] {'tp'}, dimensions={0} | all-to-all | bytes 4194304 | tf_op jit(solution)/shard_map/all_to_all | solution.py:29
  (486 shorter events, 202.8 us)
Async XLA Ops:
  6.5 67.9 %all-gather.2.cloned.1.call-start = ((), (), s32[]{:S(2)}) async-start(), calls=%async_computation.7 | async-start | bytes 1179648 | tf_op jit(solution)/shard_map/all_gather | solution.py:156
  11.4 64.7 %copy-start.31 = (s32[4]{0:T(128)}, s32[4]{0:T(128)S(1)}, u32[]{:S(2)}) copy-start(s32[4]{0:T(128)S(1)} %dynamic_slice.122) | copy-start | bytes 52
  16.0 62.0 %copy-start.36 = (f32[1,1024]{1,0:T(1,128)}, f32[1,1024]{1,0:T(1,128)S(1)}, u32[]{:S(2)}) copy-start(f32[1,1024]{1,0:T(1,128)S(1)} %get-tuple-element.511) | copy-start | bytes 12292
  78.6 21.3 %copy-start.37 = (f32[1,1024]{1,0:T(1,128)S(1)}, f32[1,1024]{1,0:T(1,128)}, u32[]{:S(2)}) copy-start(f32[1,1024]{1,0:T(1,128)} %copy-done.36) | copy-start | bytes 12292
  78.6 8.6 %collective-permute-start.3 = (bf16[1,512,256]{1,2,0:T(8,128)(2,1)S(1)}, bf16[1,512,256]{1,2,0:T(8,128)(2,1)S(1)}, u32[]{:S(2)}, u32[]{:S(2)}) collective-permute-start(bf16[1,512,256]{1,2,0:T(8,128)(2,1)S(1)} %maximum_bitcast_fusion), channel_id=1, source_target_pairs={{8,0},{16,8},{24,16},{32,24},{40,32},{48,40},{56,48},{64,56},{72,6... | collective-permute-start | bytes 786440 | tf_op jit(solution)/shard_map/ppermute | solution.py:19
  80.6 12.5 %collective-permute-start = (bf16[1,512,256]{1,2,0:T(8,128)(2,1)S(1)}, bf16[1,512,256]{1,2,0:T(8,128)(2,1)S(1)}, u32[]{:S(2)}, u32[]{:S(2)}) collective-permute-start(bf16[1,512,256]{1,2,0:T(8,128)(2,1)S(1)} %maximum_bitcast_fusion), channel_id=1, source_target_pairs={{0,8},{8,16},{16,24},{24,32},{32,40},{40,48},{48,56},{56,64},{64,7... | collective-permute-start | bytes 786440 | tf_op jit(solution)/shard_map/ppermute | solution.py:19
  86.2 62.8 %copy-start = (pred[512,512]{0,1:T(8,128)(4,1)}, pred[512,512]{0,1:T(8,128)(4,1)S(1)}, u32[]{:S(2)}) copy-start(pred[512,512]{0,1:T(8,128)(4,1)S(1)} %broadcast_compare_fusion.2) | copy-start | bytes 786436
  93.1 39.8 %collective-permute-start.4 = (bf16[2,512,256]{1,2,0:T(8,128)(2,1)S(1)}, bf16[2,512,256]{1,2,0:T(8,128)(2,1)S(1)}, u32[]{:S(2)}, u32[]{:S(2)}) collective-permute-start(bf16[2,512,256]{1,2,0:T(8,128)(2,1)S(1)} %get-tuple-element.502), channel_id=1, source_target_pairs={{16,0},{24,8},{32,16},{40,24},{48,32},{56,40},{64,48},{72,56},{80,... | collective-permute-start | bytes 1572872 | tf_op jit(solution)/shard_map/ppermute | solution.py:19
  97.1 45.2 %collective-permute-start.1 = (bf16[2,512,256]{1,2,0:T(8,128)(2,1)S(1)}, bf16[2,512,256]{1,2,0:T(8,128)(2,1)S(1)}, u32[]{:S(2)}, u32[]{:S(2)}) collective-permute-start(bf16[2,512,256]{1,2,0:T(8,128)(2,1)S(1)} %get-tuple-element.503), channel_id=1, source_target_pairs={{0,16},{8,24},{16,32},{24,40},{32,48},{40,56},{48,64},{56,72},{64,... | collective-permute-start | bytes 1572872 | tf_op jit(solution)/shard_map/ppermute | solution.py:19
  142.5 15.2 %collective-permute-start.5 = (bf16[4,512,256]{1,2,0:T(8,128)(2,1)S(1)}, bf16[4,512,256]{1,2,0:T(8,128)(2,1)S(1)}, u32[]{:S(2)}, u32[]{:S(2)}) collective-permute-start(bf16[4,512,256]{1,2,0:T(8,128)(2,1)S(1)} %get-tuple-element.500), channel_id=1, source_target_pairs={{32,0},{40,8},{48,16},{56,24},{64,32},{72,40},{80,48},{88,56},{96,... | collective-permute-start | bytes 3145736 | tf_op jit(solution)/shard_map/ppermute | solution.py:19
  145.4 16.1 %collective-permute-start.2 = (bf16[4,512,256]{1,2,0:T(8,128)(2,1)S(1)}, bf16[4,512,256]{1,2,0:T(8,128)(2,1)S(1)}, u32[]{:S(2)}, u32[]{:S(2)}) collective-permute-start(bf16[4,512,256]{1,2,0:T(8,128)(2,1)S(1)} %get-tuple-element.501), channel_id=1, source_target_pairs={{0,32},{8,40},{16,48},{24,56},{32,64},{40,72},{48,80},{56,88},{64,... | collective-permute-start | bytes 3145736 | tf_op jit(solution)/shard_map/ppermute | solution.py:19
  162.9 61.4 %copy-start.7 = (bf16[1024,128]{1,0:T(8,128)(2,1)S(1)}, bf16[1024,128]{1,0:T(8,128)(2,1)}, u32[]{:S(2)}) copy-start(bf16[1024,128]{1,0:T(8,128)(2,1)} %copy.83) | copy-start | bytes 786436
  282.9 45.6 %all-to-all-start.1 = ((f32[8,512,128]{1,2,0:T(8,128)}), f32[8,512,128]{1,2,0:T(8,128)S(1)}, u32[]{:S(2)}, u32[]{:S(2)}) async-start(f32[8,512,128]{1,2,0:T(8,128)} %broadcast_in_dim.262), calls=%async_computation.1 | async-start | bytes 4194304 | tf_op jit(solution)/shard_map/all_to_all | solution.py:35
  381.5 41.6 %all-to-all-start.3 = ((f32[8,512,128]{2,1,0:T(8,128)}), f32[8,512,128]{2,1,0:T(8,128)S(1)}, u32[]{:S(2)}, u32[]{:S(2)}) async-start(f32[8,512,128]{2,1,0:T(8,128)} %broadcast_in_dim.263), calls=%async_computation.3 | async-start | bytes 4194304 | tf_op jit(solution)/shard_map/all_to_all | solution.py:35
  429.2 14.4 %collective-permute-start.9 = (bf16[1,512,256]{1,2,0:T(8,128)(2,1)S(1)}, bf16[1,512,256]{1,2,0:T(8,128)(2,1)S(1)}, u32[]{:S(2)}, u32[]{:S(2)}) collective-permute-start(bf16[1,512,256]{1,2,0:T(8,128)(2,1)S(1)} %maximum_bitcast_fusion.1), channel_id=1, source_target_pairs={{8,0},{16,8},{24,16},{32,24},{40,32},{48,40},{56,48},{64,56},{72,6... | collective-permute-start | bytes 786440 | tf_op jit(solution)/shard_map/ppermute | solution.py:19
  437.3 13.0 %collective-permute-start.6 = (bf16[1,512,256]{1,2,0:T(8,128)(2,1)S(1)}, bf16[1,512,256]{1,2,0:T(8,128)(2,1)S(1)}, u32[]{:S(2)}, u32[]{:S(2)}) collective-permute-start(bf16[1,512,256]{1,2,0:T(8,128)(2,1)S(1)} %maximum_bitcast_fusion.1), channel_id=1, source_target_pairs={{0,8},{8,16},{16,24},{24,32},{32,40},{40,48},{48,56},{56,64},{64,7... | collective-permute-start | bytes 786440 | tf_op jit(solution)/shard_map/ppermute | solution.py:19
  441.9 16.6 %copy-start.22 = (bf16[512,2,32]{0,2,1:T(8,128)(2,1)S(1)}, bf16[512,2,32]{0,2,1:T(8,128)(2,1)}, u32[]{:S(2)}) copy-start(bf16[512,2,32]{0,2,1:T(8,128)(2,1)} %copy-done.21) | copy-start | bytes 196612
  441.9 16.6 %copy-start.24 = (bf16[512,2,32]{0,2,1:T(8,128)(2,1)S(1)}, bf16[512,2,32]{0,2,1:T(8,128)(2,1)}, u32[]{:S(2)}) copy-start(bf16[512,2,32]{0,2,1:T(8,128)(2,1)} %copy-done.23) | copy-start | bytes 196612
  443.6 53.6 %copy-start.5 = (bf16[1,512,256]{1,2,0:T(8,128)(2,1)}, bf16[1,512,256]{1,2,0:T(8,128)(2,1)S(1)}, u32[]{:S(2)}) copy-start(bf16[1,512,256]{1,2,0:T(8,128)(2,1)S(1)} %collective-permute-done.9) | copy-start | bytes 786436
  450.4 39.0 %collective-permute-start.10 = (bf16[2,512,256]{1,2,0:T(8,128)(2,1)S(1)}, bf16[2,512,256]{1,2,0:T(8,128)(2,1)S(1)}, u32[]{:S(2)}, u32[]{:S(2)}) collective-permute-start(bf16[2,512,256]{1,2,0:T(8,128)(2,1)S(1)} %get-tuple-element.498), channel_id=1, source_target_pairs={{16,0},{24,8},{32,16},{40,24},{48,32},{56,40},{64,48},{72,56},{80,... | collective-permute-start | bytes 1572872 | tf_op jit(solution)/shard_map/ppermute | solution.py:19
  452.3 44.8 %collective-permute-start.7 = (bf16[2,512,256]{1,2,0:T(8,128)(2,1)S(1)}, bf16[2,512,256]{1,2,0:T(8,128)(2,1)S(1)}, u32[]{:S(2)}, u32[]{:S(2)}) collective-permute-start(bf16[2,512,256]{1,2,0:T(8,128)(2,1)S(1)} %get-tuple-element.499), channel_id=1, source_target_pairs={{0,16},{8,24},{16,32},{24,40},{32,48},{40,56},{48,64},{56,72},{64,... | collective-permute-start | bytes 1572872 | tf_op jit(solution)/shard_map/ppermute | solution.py:19
  497.4 14.4 %collective-permute-start.11 = (bf16[4,512,256]{1,2,0:T(8,128)(2,1)S(1)}, bf16[4,512,256]{1,2,0:T(8,128)(2,1)S(1)}, u32[]{:S(2)}, u32[]{:S(2)}) collective-permute-start(bf16[4,512,256]{1,2,0:T(8,128)(2,1)S(1)} %get-tuple-element.496), channel_id=1, source_target_pairs={{32,0},{40,8},{48,16},{56,24},{64,32},{72,40},{80,48},{88,56},{96,... | collective-permute-start | bytes 3145736 | tf_op jit(solution)/shard_map/ppermute | solution.py:19
  499.4 16.1 %collective-permute-start.8 = (bf16[4,512,256]{1,2,0:T(8,128)(2,1)S(1)}, bf16[4,512,256]{1,2,0:T(8,128)(2,1)S(1)}, u32[]{:S(2)}, u32[]{:S(2)}) collective-permute-start(bf16[4,512,256]{1,2,0:T(8,128)(2,1)S(1)} %get-tuple-element.497), channel_id=1, source_target_pairs={{0,32},{8,40},{16,48},{24,56},{32,64},{40,72},{48,80},{56,88},{64,... | collective-permute-start | bytes 3145736 | tf_op jit(solution)/shard_map/ppermute | solution.py:19
  630.5 45.6 %all-to-all-start.5 = ((f32[8,512,128]{1,2,0:T(8,128)}), f32[8,512,128]{1,2,0:T(8,128)S(1)}, u32[]{:S(2)}, u32[]{:S(2)}) async-start(f32[8,512,128]{1,2,0:T(8,128)} %broadcast_in_dim.265), calls=%async_computation.5 | async-start | bytes 4194304 | tf_op jit(solution)/shard_map/all_to_all | solution.py:35
  (66 other events, 179.4 us)
Sparse Core Ops, SparseCore 0:
  9.8 64.5 all-gather.1
where the time goes:
time: 738 us; the launch traced here: 730 us
  waiting for transfers between devices  282 us (38%)
  blocking collectives  191 us (26%)
  local copies, waits for them, and re-layouts  65.2 us (9%)
  matrix products  58.2 us (8%)
  starting transfers between devices  54.9 us (7%)
  other arithmetic  46.8 us (6%)
  loops' own time  18.3 us (2%)
  between operations  14.1 us (2%)
    all_to_all x4, blocking collectives, summed_on_arrival(): lax.all_to_all(tiles, axis, split_axis=0, concat_axis=0, tiled=True)  191 us
    ppermute x12, waiting for transfers between devices, shifted(): return lax.ppermute(x, axis, pairs)  115 us
    all_to_all x3, waiting for transfers between devices, from_everyone(): lax.all_to_all(jnp.broadcast_to(x[None], (size, *x.shape)), axis, 0, 0, t...  109 us
    all_gather x1, waiting for transfers between devices, local(): whole = lax.all_gather(tokens, 'tp', axis=1, tiled=True).astype(jnp.float32)  57 us
    ppermute x12, starting transfers between devices, shifted(): return lax.ppermute(x, axis, pairs)  39.6 us
    dot_general x16, matrix products, attend(): jnp.einsum('thd,uhd->thu', query, keys, preferred_element_type=jnp.float32)  22.4 us
    dot_general x16, matrix products, attend(): jnp.einsum('thu,uhd->thd', raised.astype(jnp.bfloat16), values, preferred...  19.5 us
    another operation x2, loops' own time, local(): lax.scan(visit, state, (lower[1:reach + 1], upper[1:reach + 1], jnp.arang...  18.3 us
  transfers between devices with their start and end apart: 16, of which 16 were waited for; matrix products, arithmetic and copies ran while one was open for 4% of the time, Pallas kernels for 0%

commit v1 on v0

v1 whole, which is shorter than its diff:
```python
import functools

import jax
import jax.numpy as jnp
from jax import lax
from jax.experimental import pallas as pl
from jax.experimental.pallas import tpu as pltpu
from jax.sharding import PartitionSpec as P

HEAD_DIM = 64
BLK = 128
WINDOW = 30
CHUNK = 256

epsilon = 1e-05
theta = 10000.0
masked = -1e30
MESH = pl.DeviceIdType.MESH

AG, RS_Y, RS_Z, KV_Z, KV_FULL, KV_PART, KV_CORE, SEMS = 0, 16, 22, 24, 28, 32, 36, 44


def block_tables(block_image, image_width):
    block_total = block_image.shape[0]
    images = jnp.arange(image_width.shape[0], dtype=jnp.int32)
    member = (block_image[:, None] == images[None, :]).astype(jnp.int32)
    count = jnp.sum(member, axis=0)
    start = jnp.sum((block_image[:, None] < images[None, :]).astype(jnp.int32), axis=0)
    slots = count * BLK
    filled = slots // image_width * image_width
    first = jnp.sum(member * start[None, :], axis=1)
    return (
        first,
        jnp.sum(member * image_width[None, :], axis=1),
        jnp.sum(member * filled[None, :], axis=1),
    )


def rope_tables(first, width, first_block, shard_blocks):
    half = HEAD_DIM // 2
    offset = (first_block + jnp.arange(shard_blocks, dtype=jnp.int32) - first) * BLK
    slot = jnp.repeat(offset, BLK) + jnp.arange(shard_blocks * BLK, dtype=jnp.int32) % BLK
    width = jnp.repeat(width, BLK)
    frequency = theta ** (-2.0 * jnp.arange(half, dtype=jnp.float32) / HEAD_DIM)
    angle = jnp.concatenate(
        [
            (slot // width).astype(jnp.float32)[:, None] * frequency[None, 0::2],
            (slot % width).astype(jnp.float32)[:, None] * frequency[None, 1::2],
        ],
        axis=1,
    )
    cosine, sine = jnp.cos(angle), jnp.sin(angle)
    return (
        jnp.concatenate([cosine] * 4, axis=1),
        jnp.concatenate([-sine, sine, -sine, sine], axis=1),
    )


def normalize(values, gain):
    scale = lax.rsqrt(jnp.mean(values * values, axis=-1, keepdims=True) + epsilon)
    return (values * scale * gain).astype(jnp.bfloat16)


def rotate(heads, cosine, sine):
    lane = lax.broadcasted_iota(jnp.int32, heads.shape, 1)
    front = lax.rem(lane, HEAD_DIM) < HEAD_DIM // 2
    width = heads.shape[1]
    other = jnp.where(
        front,
        pltpu.roll(heads, width - HEAD_DIM // 2, 1),
        pltpu.roll(heads, HEAD_DIM // 2, 1),
    )
    return heads * cosine + other * sine


def layers_kernel(
    layers,
    window_ref,
    tokens_ref,
    cosine_ref,
    sine_ref,
    gain_before_ref,
    gain_after_ref,
    wq_hbm,
    wk_hbm,
    wv_hbm,
    wo_hbm,
    wg_hbm,
    wu_hbm,
    wd_hbm,
    out_ref,
    wq,
    wk,
    wv,
    wo,
    wg,
    wu,
    wd,
    whole,
    kv_first,
    kv_second,
    query,
    scores,
    attended,
    parts,
    parts_in,
    half_out,
    half_in,
    stream,
    weight_sem,
    send_sem,
    recv_sem,
):
    rows = tokens_ref.shape[0]
    blocks = rows // BLK
    row, col, tp = lax.axis_index("row"), lax.axis_index("col"), lax.axis_index("tp")
    high, low = tp // 2, tp % 2
    chip, core = row // 2, row % 2

    def at_tp(step):
        return (row, col, (high + step) % 4 * 2 + low)

    z_partner = (row, col, high * 2 + 1 - low)
    core_partner = (chip * 2 + 1 - core, col, tp)
    x_up = ((row + 2) % 8, col, tp)
    x_down = ((row + 6) % 8, col, tp)

    def at_col(step):
        return (row, (col + step) % 4, tp)

    weights = [
        pltpu.make_async_copy(src, dst, weight_sem.at[i])
        for i, (src, dst) in enumerate(
            zip(
                (wq_hbm, wk_hbm, wv_hbm, wo_hbm, wg_hbm, wu_hbm, wd_hbm),
                (wq, wk, wv, wo, wg, wu, wd),
                strict=True,
            )
        )
    ]
    for copy in weights:
        copy.start()

    barrier = pltpu.get_barrier_semaphore()
    peers = [at_tp(1), at_tp(2), at_tp(3), z_partner, core_partner, x_up, x_down]
    peers += [at_col(1), at_col(2), at_col(3)]
    for peer in peers:
        pl.semaphore_signal(barrier, inc=1, device_id=peer, device_id_type=MESH)
    pl.semaphore_wait(barrier, len(peers))

    stream[...] = tokens_ref[...].astype(jnp.float32)
    for copy in weights:
        copy.wait()

    def layer_body(layer):
        def send(src, dst, sem, device):
            return pltpu.make_async_remote_copy(
                src_ref=src,
                dst_ref=dst,
                send_sem=send_sem.at[layer, sem],
                recv_sem=recv_sem.at[layer, sem],
                device_id=device,
                device_id_type=MESH,
            )

        def gather(stage):
            held = whole.at[layer, stage]
            base = AG + 8 * stage
            held[tp] = stream[...].astype(jnp.bfloat16)
            sent = [send(held.at[tp], held.at[tp], base + 3, z_partner)]
            sent += [send(held.at[tp], held.at[tp], base + d - 1, at_tp(d)) for d in (1, 3, 2)]
            for copy in sent:
                copy.start()
            other = tp + 1 - 2 * low
            sent[0].wait_recv()
            passed = [send(held.at[other], held.at[other], base + 3 + d, at_tp(d)) for d in (1, 3, 2)]
            for copy in passed:
                copy.start()
            for copy in sent[1:] + passed:
                copy.wait_recv()
            for copy in sent + passed:
                copy.wait_send()

        def scatter(stage):
            own = parts.at[layer, stage]
            arrived = parts_in.at[layer, stage]
            base = RS_Y + 3 * stage
            sent = [
                send(
                    own.at[pl.ds((high + d) % 4 * 2, 2)],
                    arrived.at[d - 1],
                    base + d - 1,
                    at_tp(d),
                )
                for d in (1, 3, 2)
            ]
            for copy in sent:
                copy.start()
            for copy in sent:
                copy.wait()

            def summed(half):
                total = own[high * 2 + half].astype(jnp.float32)
                for d in range(3):
                    total = total + arrived[d, half].astype(jnp.float32)
                return total

            half_out[layer, stage] = summed(1 - low).astype(jnp.bfloat16)
            cross = send(half_out.at[layer, stage], half_in.at[layer, stage], RS_Z + stage, z_partner)
            cross.start()
            stream[...] = stream[...] + summed(low)
            cross.wait()
            stream[...] = stream[...] + half_in[layer, stage].astype(jnp.float32)

        def whole_block(stage, at):
            return jnp.concatenate(
                [whole[layer, stage, i, at, :] for i in range(8)], axis=1
            ).astype(jnp.float32)

        held_kv = (kv_first, kv_second)[layer]

        def shard(offset, number):
            return held_kv.at[pl.ds((offset * 8 + number) * blocks, blocks)]

        gather(0)

        def project(block, unused):
            at = pl.ds(pl.multiple_of(block * BLK, BLK), BLK)
            normed = normalize(
                whole_block(0, at), gain_before_ref[layer].astype(jnp.float32)
            )
            cosine, sine = cosine_ref[at, :], sine_ref[at, :]
            turned = rotate(
                jnp.dot(normed, wq[layer], preferred_element_type=jnp.float32), cosine, sine
            ).astype(jnp.bfloat16)
            query[at, :] = turned * jnp.bfloat16(HEAD_DIM**-0.5)
            here = (8 + core * 4 + col) * blocks + block
            held_kv[here, :, 0:BLK] = rotate(
                jnp.dot(normed, wk[layer], preferred_element_type=jnp.float32), cosine, sine
            ).astype(jnp.bfloat16)
            held_kv[here, :, BLK : 2 * BLK] = jnp.dot(
                normed, wv[layer], preferred_element_type=jnp.float32
            ).astype(jnp.bfloat16)
            return unused

        lax.fori_loop(0, blocks, project, 0)

        own_number = core * 4 + col
        along = [
            send(shard(1, own_number), shard(1, own_number), KV_Z + d, at_col(d)) for d in (1, 3, 2)
        ]
        for copy in along:
            copy.start()
        full_slot = 2 - 2 * core
        part_slot = 2 * core
        started = []

        def to_full(source):
            there = ((row + 6 + 4 * core) % 8, col, tp)
            return send(
                shard(1, core * 4 + source), shard(full_slot, core * 4 + source), KV_FULL + source, there
            )

        def to_part(source):
            there = ((row + 2 + 4 * core) % 8, col, tp)
            return send(
                shard(1, core * 4 + source), shard(part_slot, core * 4 + source), KV_PART + source, there
            )

        def part_needed(source):
            return ((core == 0) & (source > col)) | ((core == 1) & (source < col))

        def to_core(slot, source, sem):
            number = core * 4 + source
            return send(shard(slot, number), shard(slot, number), KV_CORE + sem + source, core_partner)

        for d in (0, 1, 3, 2):
            source = (col + 4 - d) % 4
            if d:
                send(shard(1, own_number), shard(1, own_number), KV_Z + d, at_col(d)).wait_recv()

                @pl.when(part_needed(source))
                def _():
                    to_part(source).start()

            to_full(source).start()
            to_core(1, source, 0).start()
        for d in (0, 1, 3, 2):
            source = (col + 4 - d) % 4
            to_full(source).wait_recv()
            to_core(full_slot, source, 4).start()
        for d in (0, 1, 3, 2):
            source = (col + 4 - d) % 4
            to_full(source).wait_send()
            if d:

                @pl.when(part_needed(source))
                def _():
                    to_part(source).wait()

            to_core(1, source, 0).wait()
            to_core(full_slot, source, 4).wait()
        for copy in along:
            copy.wait_send()

        lane = lax.broadcasted_iota(jnp.int32, (BLK, BLK), 1)
        chunks = WINDOW * BLK // CHUNK
        each = CHUNK // BLK

        def keys_of(begin, chunk, lanes):
            return jnp.concatenate(
                [held_kv[begin + chunk * each + i][:, lanes : lanes + BLK] for i in range(each)], axis=0
            )

        def attend(block, unused):
            at = pl.ds(pl.multiple_of(block * BLK, BLK), BLK)
            begin = window_ref[block, 0]
            shift = window_ref[block, 1]
            filled = window_ref[block, 2]
            turned = query[at, :]
            zero = jnp.zeros_like(turned)
            stacked = jnp.concatenate(
                [jnp.where(lane < HEAD_DIM, turned, zero), jnp.where(lane < HEAD_DIM, zero, turned)],
                axis=0,
            )
            best = jnp.full((2 * BLK, BLK), masked, jnp.float32)
            for chunk in range(chunks):
                keys = keys_of(begin, chunk, 0)
                found = lax.dot_general(
                    stacked, keys, (((1,), (1,)), ((), ())), preferred_element_type=jnp.float32
                )
                slot = lax.broadcasted_iota(jnp.int32, (1, CHUNK), 1) + (shift + chunk * CHUNK)
                found = jnp.where((slot >= 0) & (slot < filled), found, masked)
                scores[:, chunk * CHUNK : (chunk + 1) * CHUNK] = found
                for part in range(CHUNK // BLK):
                    best = jnp.maximum(best, found[:, part * BLK : (part + 1) * BLK])
            top = jnp.max(best, axis=1, keepdims=True)
            total = jnp.zeros((2 * BLK, BLK), jnp.float32)
            mixed = jnp.zeros((2 * BLK, BLK), jnp.float32)
            for chunk in range(chunks):
                raised = jnp.exp(scores[:, chunk * CHUNK : (chunk + 1) * CHUNK] - top)
                for part in range(CHUNK // BLK):
                    total = total + raised[:, part * BLK : (part + 1) * BLK]
                values = keys_of(begin, chunk, BLK)
                mixed = mixed + jnp.dot(
                    raised.astype(jnp.bfloat16), values, preferred_element_type=jnp.float32
                )
            mixed = mixed / jnp.sum(total, axis=1, keepdims=True)
            attended[at, :] = jnp.where(lane < HEAD_DIM, mixed[0:BLK], mixed[BLK:]).astype(
                jnp.bfloat16
            )
            return unused

        lax.fori_loop(0, blocks, attend, 0)

        def spread(stage, at, part):
            for i in range(8):
                parts[layer, stage, i, at, :] = part[:, i * BLK : (i + 1) * BLK].astype(jnp.bfloat16)

        def project_out(block, unused):
            at = pl.ds(pl.multiple_of(block * BLK, BLK), BLK)
            spread(0, at, jnp.dot(attended[at, :], wo[layer], preferred_element_type=jnp.float32))
            return unused

        lax.fori_loop(0, blocks, project_out, 0)
        scatter(0)
        gather(1)

        def feed(block, unused):
            at = pl.ds(pl.multiple_of(block * 2 * BLK, BLK), 2 * BLK)
            post = normalize(whole_block(1, at), gain_after_ref[layer].astype(jnp.float32))
            gate = jnp.dot(post, wg[layer], preferred_element_type=jnp.float32)
            up = jnp.dot(post, wu[layer], preferred_element_type=jnp.float32)
            hidden = (gate / (1.0 + jnp.exp(-gate)) * up).astype(jnp.bfloat16)
            spread(1, at, jnp.dot(hidden, wd[layer], preferred_element_type=jnp.float32))
            return unused

        lax.fori_loop(0, blocks // 2, feed, 0)
        scatter(1)

    for layer in range(layers):
        layer_body(layer)
    out_ref[...] = stream[...]


def local(
    tokens,
    norm_before,
    query_weight,
    key_weight,
    value_weight,
    output_weight,
    norm_after,
    gate_weight,
    up_weight,
    down_weight,
    block_image,
    image_width,
):
    rows = tokens.shape[0]
    blocks = rows // BLK
    layers = query_weight.shape[0]
    place = lax.axis_index(("row", "col"))
    first, width, filled = [
        lax.dynamic_slice_in_dim(table, place * blocks, blocks)
        for table in block_tables(block_image, image_width)
    ]
    cosine, sine = rope_tables(first, width, place * blocks, blocks)
    origin = (place // 8 - 1) * 8 * blocks
    begin = jnp.minimum(first, place * blocks + 8 * blocks - WINDOW)
    window = jnp.stack([begin - origin, (begin - first) * BLK, filled], axis=1)
    hbm = pl.BlockSpec(memory_space=pl.ANY)
    vmem = pl.BlockSpec(memory_space=pltpu.VMEM)
    bf16, f32 = jnp.bfloat16, jnp.float32
    return pl.pallas_call(
        functools.partial(layers_kernel, layers),
        out_shape=jax.ShapeDtypeStruct(tokens.shape, f32),
        in_specs=[pl.BlockSpec(memory_space=pltpu.SMEM)] + [vmem] * 5 + [hbm] * 7,
        out_specs=vmem,
        scratch_shapes=[
            pltpu.VMEM(w.shape, bf16)
            for w in (
                query_weight,
                key_weight,
                value_weight,
                output_weight,
                gate_weight,
                up_weight,
                down_weight,
            )
        ]
        + [
            pltpu.VMEM((layers, 2, 8, rows, BLK), bf16),
            pltpu.VMEM((24 * blocks, BLK, 2 * BLK), bf16),
            pltpu.VMEM((24 * blocks, BLK, 2 * BLK), bf16),
            pltpu.VMEM((rows, BLK), bf16),
            pltpu.VMEM((2 * BLK, WINDOW * BLK), f32),
            pltpu.VMEM((rows, BLK), bf16),
            pltpu.VMEM((layers, 2, 8, rows, BLK), bf16),
            pltpu.VMEM((layers, 2, 3, 2, rows, BLK), bf16),
            pltpu.VMEM((layers, 2, rows, BLK), bf16),
            pltpu.VMEM((layers, 2, rows, BLK), bf16),
            pltpu.VMEM((rows, BLK), f32),
            pltpu.SemaphoreType.DMA((7,)),
            pltpu.SemaphoreType.DMA((layers, SEMS)),
            pltpu.SemaphoreType.DMA((layers, SEMS)),
        ],
        compiler_params=pltpu.CompilerParams(
            collective_id=0, has_side_effects=True, vmem_limit_bytes=56 << 20
        ),
        name="encoder_layers",
    )(
        window,
        tokens,
        cosine,
        sine,
        norm_before[:, None, :],
        norm_after[:, None, :],
        query_weight,
        key_weight,
        value_weight,
        output_weight,
        gate_weight,
        up_weight,
        down_weight,
    )


def solution(mesh):
    placed = (
        P(("row", "col"), "tp"),
        P(),
        P(None, None, "tp"),
        P(None, None, "tp"),
        P(None, None, "tp"),
        P(None, "tp", None),
        P(),
        P(None, None, "tp"),
        P(None, None, "tp"),
        P(None, "tp", None),
        P(),
        P(),
    )
    return jax.shard_map(
        local, mesh=mesh, in_specs=placed, out_specs=P(("row", "col"), "tp"), check_vma=False
    )
```

time: 738 us -> 252 us (0.34)
  waiting for transfers between devices: 282 us -> 0 us
  Pallas kernels: 0 us -> 239 us
  blocking collectives: 191 us -> 0 us
  local copies, waits for them, and re-layouts: 65.2 us -> 3.76 us
  matrix products: 58.2 us -> 0 us
  starting transfers between devices: 54.9 us -> 0 us
  other arithmetic: 46.8 us -> 6.42 us
  loops' own time: 18.3 us -> 0 us
  between operations: 14.1 us -> 0.06 us
    pallas_call x0 -> x1, Pallas kernels: none -> 239 us  [local(): pl.pallas_call(functools.partial(layers_kernel, layers), out_shape=jax.Sh...]
    all_to_all x4 -> x0, blocking collectives: 191 us -> none  [summed_on_arrival(): lax.all_to_all(tiles, axis, split_axis=0, concat_axis=0, tiled=True)]
    ppermute x12 -> x0, waiting for transfers between devices: 115 us -> none  [shifted(): return lax.ppermute(x, axis, pairs)]
    all_to_all x3 -> x0, waiting for transfers between devices: 109 us -> none  [from_everyone(): lax.all_to_all(jnp.broadcast_to(x[None], (size, *x.shape)), axis, 0, 0, t...]
    dot_general x44 -> x0, matrix products: 58.2 us -> none  [the longest x16 22.4 us: attend(): jnp.einsum('thd,uhd->thu', query, keys, preferred_element_type=jnp.float32)]
    all_gather x1 -> x0, waiting for transfers between devices: 57 us -> none  [local(): whole = lax.all_gather(tokens, 'tp', axis=1, tiled=True).astype(jnp.float32)]
    ppermute x12 -> x0, starting transfers between devices: 39.6 us -> none  [shifted(): return lax.ppermute(x, axis, pairs)]
    reduce_sum x25 -> x1, other arithmetic: 19.6 us -> 0.87 us  [block_tables(): jnp.sum(member * image_width[None, :], axis=1)]
  transfers between devices with their start and end apart: 16 -> 0, of which waited for: 16 -> 0; matrix products, arithmetic and copies ran while one was open for 4% -> 0% of each run, Pallas kernels for 0% -> 0%
where the time goes in v1:
time: 252 us; the launch traced here: 249 us
  Pallas kernels  239 us (95%)
  other arithmetic  6.42 us (3%)
  local copies, waits for them, and re-layouts  3.76 us (1%)
    pallas_call x1, Pallas kernels, local(): pl.pallas_call(functools.partial(layers_kernel, layers), out_shape=jax.Sh...  239 us

profile of v1, /device:TPU:4, one launch (start us, length us, event | category | flops | bytes accessed | tf_op | source)
XLA Modules:
  0.0 249.3 jit_solution(9547385670614047337)
XLA Ops:
  0.0 0.8 convert_reduce_fusion
  0.8 0.8 fusion.17
  1.6 0.9 select_reduce_fusion
  2.5 0.7 select_reduce_fusion.2
  3.2 0.1 subtract_multiply_fusion
  3.3 0.1 dynamic_slice.11
  3.3 0.2 fusion.12
  3.6 0.1 slice.6
  3.7 0.1 slice.7
  3.8 0.1 broadcast_multiply_fusion
  3.9 0.2 fusion
  4.1 0.1 copy.42
  4.3 1.0 pad_maximum_fusion.1.sine_ref
  5.2 0.1 copy.38
  5.4 1.0 pad_maximum_fusion.cosine_ref
  6.3 0.1 copy.35
  6.4 0.1 copy.36
  6.5 0.1 dynamic-slice_bitcast_fusion
  6.6 0.1 copy.37
  6.7 0.7 pad_add_fusion.window_ref
  7.4 0.6 copy.45.gain_before_ref
  8.0 0.6 copy.46.gain_after_ref
  8.6 239.1 %encoder_layers.1 = f32[512,128]{1,0:T(8,128)} custom-call(s32[4,3]{1,0:T(4,128)} %pad_add_fusion.window_ref, bf16[512,128]{1,0:T(8,128)(2,1)} %tokens_ref.1, f32[512,128]{1,0:T(8,128)} %pad_maximum_fusion.cosine_ref, f32[512,128]{1,0:T(8,128)} %pad_maximum_fusion.1.sine_ref, bf16[2,1,1024]{2,1,0:T(2,128)(2,1)} %copy.45.gain_before_ref, ...), custom_call_target="tpu_custom_call" | custom-call | tf_op jit(solution)/shard_map/encoder_layers/pallas_call | solution.py:415
  247.7 1.7 copy.48
  (6 shorter events, 0.0 us)
Async XLA Ops:
  0.0 7.4 %copy-start = (bf16[2,1024]{1,0:T(2,128)(2,1)S(1)}, bf16[2,1024]{1,0:T(2,128)(2,1)}, u32[]{:S(2)}) copy-start(bf16[2,1024]{1,0:T(2,128)(2,1)} %param.13) | copy-start | bytes 12292
  0.0 8.0 %copy-start.1 = (bf16[2,1024]{1,0:T(2,128)(2,1)S(1)}, bf16[2,1024]{1,0:T(2,128)(2,1)}, u32[]{:S(2)}) copy-start(bf16[2,1024]{1,0:T(2,128)(2,1)} %param.18) | copy-start | bytes 12292

commit v2 on v1

v2 whole, which is shorter than its diff:
```python
import functools

import jax
import jax.numpy as jnp
from jax import lax
from jax.experimental import pallas as pl
from jax.experimental.pallas import tpu as pltpu
from jax.sharding import PartitionSpec as P

HEAD_DIM = 64
BLK = 128
WINDOW = 30
CHUNK = 256

epsilon = 1e-05
theta = 10000.0
masked = -1e30
MESH = pl.DeviceIdType.MESH

UNIT = 2

AG_X, AG_A, RS_Y, OUT_W, KV = 0, 32, 64, 80, 96
KV_UP, KV_DOWN, KV_FULL, KV_PART, KV_CORE, KV_BACK, KV_SEMS = 0, 4, 8, 12, 16, 20, 24
SEMS = KV + 2 * KV_SEMS


def block_tables(block_image, image_width):
    block_total = block_image.shape[0]
    images = jnp.arange(image_width.shape[0], dtype=jnp.int32)
    member = (block_image[:, None] == images[None, :]).astype(jnp.int32)
    count = jnp.sum(member, axis=0)
    start = jnp.sum((block_image[:, None] < images[None, :]).astype(jnp.int32), axis=0)
    slots = count * BLK
    filled = slots // image_width * image_width
    first = jnp.sum(member * start[None, :], axis=1)
    return (
        first,
        jnp.sum(member * image_width[None, :], axis=1),
        jnp.sum(member * filled[None, :], axis=1),
    )


def rope_tables(first, width, first_block, shard_blocks):
    half = HEAD_DIM // 2
    offset = (first_block + jnp.arange(shard_blocks, dtype=jnp.int32) - first) * BLK
    slot = jnp.repeat(offset, BLK) + jnp.arange(shard_blocks * BLK, dtype=jnp.int32) % BLK
    width = jnp.repeat(width, BLK)
    frequency = theta ** (-2.0 * jnp.arange(half, dtype=jnp.float32) / HEAD_DIM)
    angle = jnp.concatenate(
        [
            (slot // width).astype(jnp.float32)[:, None] * frequency[None, 0::2],
            (slot % width).astype(jnp.float32)[:, None] * frequency[None, 1::2],
        ],
        axis=1,
    )
    cosine, sine = jnp.cos(angle), jnp.sin(angle)
    return (
        jnp.concatenate([cosine] * 4, axis=1),
        jnp.concatenate([-sine, sine, -sine, sine], axis=1),
    )


def normalize(values, gain):
    scale = lax.rsqrt(jnp.mean(values * values, axis=-1, keepdims=True) + epsilon)
    return (values * scale * gain).astype(jnp.bfloat16)


def rotate(heads, cosine, sine):
    lane = lax.broadcasted_iota(jnp.int32, heads.shape, 1)
    front = lax.rem(lane, HEAD_DIM) < HEAD_DIM // 2
    width = heads.shape[1]
    other = jnp.where(
        front,
        pltpu.roll(heads, width - HEAD_DIM // 2, 1),
        pltpu.roll(heads, HEAD_DIM // 2, 1),
    )
    return heads * cosine + other * sine


def layers_kernel(
    layers,
    window_ref,
    tokens_ref,
    cosine_ref,
    sine_ref,
    gain_before_ref,
    gain_after_ref,
    wq_hbm,
    wk_hbm,
    wv_hbm,
    wo_hbm,
    wg_hbm,
    wu_hbm,
    wd_hbm,
    out_ref,
    wq,
    wk,
    wv,
    wo,
    wg,
    wu,
    wd,
    inputs,
    mixes,
    kv_first,
    kv_second,
    query,
    scores,
    head_part,
    parts,
    parts_in,
    half_out,
    half_in,
    stream,
    weight_sem,
    send_sem,
    recv_sem,
):
    rows = tokens_ref.shape[0]
    blocks = rows // BLK
    row, col, tp = lax.axis_index("row"), lax.axis_index("col"), lax.axis_index("tp")
    high, low = tp // 2, tp % 2
    chip, core = row // 2, row % 2
    other = high * 2 + 1 - low

    def at_tp(step):
        return (row, col, (high + step) % 4 * 2 + low)

    z_partner = (row, col, other)
    core_partner = (chip * 2 + 1 - core, col, tp)
    x_full = ((row + 6 + 4 * core) % 8, col, tp)
    x_part = ((row + 2 + 4 * core) % 8, col, tp)
    z_up = (row, (col + 1) % 4, tp)
    z_down = (row, (col + 3) % 4, tp)

    own_out_rows = pl.ds(pl.multiple_of(tp * BLK, BLK), BLK)
    weights = [
        pltpu.make_async_copy(src, dst, weight_sem.at[i])
        for i, (src, dst) in enumerate(
            [(wo_hbm.at[i], wo.at[i, own_out_rows]) for i in range(layers)]
            + [(wq_hbm, wq), (wk_hbm, wk), (wv_hbm, wv), (wg_hbm, wg), (wu_hbm, wu), (wd_hbm, wd)]
        )
    ]
    for copy in weights:
        copy.start()

    barrier = pltpu.get_barrier_semaphore()
    peers = [at_tp(1), at_tp(2), at_tp(3), z_partner, core_partner, x_full, x_part, z_up, z_down]
    for peer in peers:
        pl.semaphore_signal(barrier, inc=1, device_id=peer, device_id_type=MESH)
    pl.semaphore_wait(barrier, len(peers))

    pending = []

    def send(src, dst, layer, sem, device):
        return pltpu.make_async_remote_copy(
            src_ref=src,
            dst_ref=dst,
            send_sem=send_sem.at[layer, sem],
            recv_sem=recv_sem.at[layer, sem],
            device_id=device,
            device_id_type=MESH,
        )

    def go(copy):
        copy.start()
        pending.append((None, copy))

    def drain():
        for needed, copy in pending:
            if needed is None:
                copy.wait_send()
            else:

                @pl.when(needed)
                def _(copy=copy):
                    copy.wait_send()

        pending.clear()

    def span(chunk):
        return pl.ds(chunk * BLK, BLK)

    def gather_own(held, layer, base, chunk):
        piece = held.at[tp, span(chunk)]
        go(send(piece, piece, layer, base + 8 * chunk, z_partner))
        for d in (1, 3, 2):
            go(send(piece, piece, layer, base + 8 * chunk + d, at_tp(d)))

    def gather_pass(held, layer, base, chunk):
        piece = held.at[other, span(chunk)]
        send(piece, piece, layer, base + 8 * chunk, z_partner).wait_recv()
        for d in (1, 3, 2):
            go(send(piece, piece, layer, base + 8 * chunk + 3 + d, at_tp(d)))

    def gather_end(held, layer, base, chunk):
        piece = held.at[tp, span(chunk)]
        for d in (1, 3, 2):
            send(piece, piece, layer, base + 8 * chunk + d, at_tp(d)).wait_recv()
        for d in (1, 3, 2):
            send(piece, piece, layer, base + 8 * chunk + 3 + d, at_tp(d)).wait_recv()

    def whole_rows(held, chunk):
        return jnp.concatenate([held[i, span(chunk), :] for i in range(8)], axis=1)

    def out_half(layer, number):
        return wo.at[layer, pl.ds(pl.multiple_of(number * BLK + core * (BLK // 2), 64), BLK // 2)]

    def out_cross(layer):
        weights[layer].wait()
        go(send(out_half(layer, tp), out_half(layer, tp), layer, OUT_W, z_partner))

    def out_own(layer):
        for d in (1, 3, 2):
            go(send(out_half(layer, tp), out_half(layer, tp), layer, OUT_W + d, at_tp(d)))

    def out_core(layer, number, sem):
        go(send(out_half(layer, number), out_half(layer, number), layer, OUT_W + 8 + sem, core_partner))

    def out_pass(layer):
        send(out_half(layer, tp), out_half(layer, tp), layer, OUT_W, z_partner).wait_recv()
        for d in (1, 3, 2):
            go(send(out_half(layer, other), out_half(layer, other), layer, OUT_W + 3 + d, at_tp(d)))
        out_core(layer, other, 0)

    def out_share(layer):
        for d in (1, 3, 2):
            held = out_half(layer, tp)
            send(held, held, layer, OUT_W + d, at_tp(d)).wait_recv()
            out_core(layer, (high + 4 - d) % 4 * 2 + low, d)
            send(held, held, layer, OUT_W + 3 + d, at_tp(d)).wait_recv()
            out_core(layer, (high + 4 - d) % 4 * 2 + 1 - low, 3 + d)

    def out_end(layer):
        held = out_half(layer, tp)
        for i in range(7):
            send(held, held, layer, OUT_W + 8 + i, core_partner).wait_recv()

    def start_layer(layer, chunk):
        inputs[layer, tp, span(chunk), :] = stream[span(chunk), :].astype(jnp.bfloat16)
        gather_own(inputs.at[layer], layer, AG_X, chunk)

    def pass_layer(layer, chunk):
        gather_pass(inputs.at[layer], layer, AG_X, chunk)

    def project(layer, chunk):
        gather_end(inputs.at[layer], layer, AG_X, chunk)
        held_kv = (kv_first, kv_second)[layer]
        at = span(chunk)
        normed = normalize(
            whole_rows(inputs.at[layer], chunk).astype(jnp.float32),
            gain_before_ref[layer].astype(jnp.float32),
        )
        cosine, sine = cosine_ref[at, :], sine_ref[at, :]
        here = (8 + core * 4 + col) * blocks + chunk
        held_kv[here, :, 0:BLK] = rotate(
            jnp.dot(normed, wk[layer], preferred_element_type=jnp.float32), cosine, sine
        ).astype(jnp.bfloat16)
        held_kv[here, :, BLK : 2 * BLK] = jnp.dot(
            normed, wv[layer], preferred_element_type=jnp.float32
        ).astype(jnp.bfloat16)
        if chunk % UNIT == UNIT - 1:
            spread_own(layer, chunk // UNIT)
        turned = rotate(
            jnp.dot(normed, wq[layer], preferred_element_type=jnp.float32), cosine, sine
        ).astype(jnp.bfloat16)
        query[at, :] = turned * jnp.bfloat16(HEAD_DIM**-0.5)
        if chunk == blocks - 1:
            out_own(layer)
            out_pass(layer)

    def kv_unit(layer, offset, source, unit):
        number = (offset * 8 + core * 4 + source) * blocks + unit * UNIT
        return (kv_first, kv_second)[layer].at[pl.ds(number, UNIT)]

    def kv_send(layer, unit, kind, source, device, slot=None):
        slot = 1 if slot is None else slot
        target = {KV_FULL: 2 - 2 * core, KV_PART: 2 * core}.get(kind, slot)
        return send(
            kv_unit(layer, slot, source, unit),
            kv_unit(layer, target, source, unit),
            layer,
            KV + unit * KV_SEMS + kind + source,
            device,
        )

    def spread_shard(layer, unit, source):
        kv_send(layer, unit, KV_FULL, source, x_full).start()
        kv_send(layer, unit, KV_CORE, source, core_partner).start()
        pending.append((None, kv_send(layer, unit, KV_FULL, source, x_full)))
        pending.append((None, kv_send(layer, unit, KV_CORE, source, core_partner)))

    def spread_own(layer, unit):
        for kind, device, needed in ((KV_UP, z_up, col < 3), (KV_DOWN, z_down, col > 0)):
            copy = kv_send(layer, unit, kind, col, device)

            @pl.when(needed)
            def _(copy=copy):
                copy.start()

            pending.append((needed, copy))
        spread_shard(layer, unit, col)

    def spread_next(layer, unit, step):
        for kind, source, device, here, onward, part in (
            (KV_UP, col - step, z_up, col >= step, col < 3, core == 1),
            (KV_DOWN, col + step, z_down, col + step <= 3, col > 0, core == 0),
        ):
            arrived = kv_send(layer, unit, kind, source, device)
            aside = kv_send(layer, unit, KV_PART, source, x_part)
            full = kv_send(layer, unit, KV_FULL, source, x_full)
            across = kv_send(layer, unit, KV_CORE, source, core_partner)

            @pl.when(here)
            def _(arrived=arrived, aside=aside, full=full, across=across, onward=onward, part=part):
                arrived.wait_recv()

                @pl.when(onward)
                def _():
                    arrived.start()

                full.start()

                @pl.when(part)
                def _():
                    aside.start()

                across.start()

            pending.append((here & onward, arrived))
            pending.append((here & part, aside))
            pending.append((here, full))
            pending.append((here, across))

    def order_of(step):
        return (col + step) % 4

    def spread_back(layer, unit):
        for step in (0, 1, 3, 2):
            source = order_of(step)
            kv_send(layer, unit, KV_FULL, source, x_full).wait_recv()
            go(kv_send(layer, unit, KV_BACK, source, core_partner, slot=2 - 2 * core))

    def spread_end(layer, unit):
        for step in (1, 2, 3):
            source = order_of(step)

            @pl.when(((core == 0) & (source > col)) | ((core == 1) & (source < col)))
            def _(source=source):
                kv_send(layer, unit, KV_PART, source, x_part).wait_recv()

        for source in range(4):
            kv_send(layer, unit, KV_CORE, source, core_partner).wait_recv()
            kv_send(layer, unit, KV_BACK, source, core_partner).wait_recv()

    lane = lax.broadcasted_iota(jnp.int32, (BLK, BLK), 1)
    chunks = WINDOW * BLK // CHUNK
    each = CHUNK // BLK

    def attend(layer, block):
        held_kv = (kv_first, kv_second)[layer]

        def keys_of(begin, chunk, lanes):
            return jnp.concatenate(
                [held_kv[begin + chunk * each + i][:, lanes : lanes + BLK] for i in range(each)], axis=0
            )

        at = span(block)
        begin = window_ref[block, 0]
        shift = window_ref[block, 1]
        filled = window_ref[block, 2]
        turned = query[at, :]
        zero = jnp.zeros_like(turned)
        stacked = jnp.concatenate(
            [jnp.where(lane < HEAD_DIM, turned, zero), jnp.where(lane < HEAD_DIM, zero, turned)],
            axis=0,
        )
        best = jnp.full((2 * BLK, BLK), masked, jnp.float32)
        for chunk in range(chunks):
            found = lax.dot_general(
                stacked,
                keys_of(begin, chunk, 0),
                (((1,), (1,)), ((), ())),
                preferred_element_type=jnp.float32,
            )
            slot = lax.broadcasted_iota(jnp.int32, (1, CHUNK), 1) + (shift + chunk * CHUNK)
            found = jnp.where((slot >= 0) & (slot < filled), found, masked)
            scores[:, chunk * CHUNK : (chunk + 1) * CHUNK] = found
            for part in range(each):
                best = jnp.maximum(best, found[:, part * BLK : (part + 1) * BLK])
        top = jnp.max(best, axis=1, keepdims=True)
        total = jnp.zeros((2 * BLK, BLK), jnp.float32)
        mixed = jnp.zeros((2 * BLK, BLK), jnp.float32)
        for chunk in range(chunks):
            raised = jnp.exp(scores[:, chunk * CHUNK : (chunk + 1) * CHUNK] - top)
            for part in range(each):
                total = total + raised[:, part * BLK : (part + 1) * BLK]
            mixed = mixed + jnp.dot(
                raised.astype(jnp.bfloat16),
                keys_of(begin, chunk, BLK),
                preferred_element_type=jnp.float32,
            )
        mixed = mixed / jnp.sum(total, axis=1, keepdims=True)
        mixes[layer, tp, at, :] = jnp.where(lane < HEAD_DIM, mixed[0:BLK], mixed[BLK:]).astype(
            jnp.bfloat16
        )
        gather_own(mixes.at[layer], layer, AG_A, block)

    def pass_mix(layer, chunk):
        gather_pass(mixes.at[layer], layer, AG_A, chunk)

    def feed(layer, chunk):
        if chunk == 0:
            out_end(layer)
        gather_end(mixes.at[layer], layer, AG_A, chunk)
        at = span(chunk)
        headed = jnp.dot(
            whole_rows(mixes.at[layer], chunk), wo[layer], preferred_element_type=jnp.float32
        )
        for i in range(8):
            head_part[i] = headed[:, i * BLK : (i + 1) * BLK]
        stream[at, :] = stream[at, :] + head_part[tp]
        middle = whole_rows(inputs.at[layer], chunk).astype(jnp.float32) + headed
        post = normalize(middle, gain_after_ref[layer].astype(jnp.float32))
        gate = jnp.dot(post, wg[layer], preferred_element_type=jnp.float32)
        up = jnp.dot(post, wu[layer], preferred_element_type=jnp.float32)
        hidden = (gate / (1.0 + jnp.exp(-gate)) * up).astype(jnp.bfloat16)
        part = jnp.dot(hidden, wd[layer], preferred_element_type=jnp.float32)
        for i in range(8):
            parts[layer, i, at, :] = part[:, i * BLK : (i + 1) * BLK].astype(jnp.bfloat16)
        for d in (1, 3, 2):
            go(sum_send(layer, chunk, d))
        if chunk == 0 and layer + 1 < layers:
            out_cross(layer + 1)

    def sum_send(layer, chunk, d):
        return send(
            parts.at[layer, pl.ds((high + d) % 4 * 2, 2), span(chunk)],
            parts_in.at[layer, d - 1, pl.ds(0, 2), span(chunk)],
            layer,
            RS_Y + 4 * chunk + d,
            at_tp(d),
        )

    def cross_send(layer, chunk):
        return send(
            half_out.at[layer, span(chunk)],
            half_in.at[layer, span(chunk)],
            layer,
            RS_Y + 4 * chunk,
            z_partner,
        )

    def add_up(layer, chunk):
        at = span(chunk)
        for d in (1, 3, 2):
            sum_send(layer, chunk, d).wait_recv()

        def summed(half):
            total = parts[layer, high * 2 + half, at, :].astype(jnp.float32)
            for d in range(3):
                total = total + parts_in[layer, d, half, at, :].astype(jnp.float32)
            return total

        half_out[layer, at, :] = summed(1 - low).astype(jnp.bfloat16)
        go(cross_send(layer, chunk))
        stream[at, :] = stream[at, :] + summed(low)

    def finish(layer, chunk):
        at = span(chunk)
        cross_send(layer, chunk).wait_recv()
        stream[at, :] = stream[at, :] + half_in[layer, at, :].astype(jnp.float32)
        if layer + 1 < layers:
            start_layer(layer + 1, chunk)

    def in_units(stage):
        def run(layer, chunk):
            if chunk % UNIT == UNIT - 1:
                stage(layer, chunk // UNIT)

        return run

    def wavefront(stages):
        for step in range(blocks + len(stages) - 1):
            for i in reversed(range(len(stages))):
                if 0 <= step - i < blocks:
                    layer, stage = stages[i]
                    stage(layer, step - i)

    def chain(step):
        return in_units(lambda layer, unit: spread_next(layer, unit, step))

    def front(layer):
        return [
            (layer, pass_layer),
            (layer, project),
            (layer, chain(1)),
            (layer, chain(2)),
            (layer, chain(3)),
            (layer, in_units(spread_back)),
        ]

    def rest(layer):
        return [(layer, attend), (layer, pass_mix), (layer, feed), (layer, add_up), (layer, finish)]

    stream[...] = tokens_ref[...].astype(jnp.float32)
    for chunk in range(blocks):
        start_layer(0, chunk)
    out_cross(0)
    for copy in weights[layers:]:
        copy.wait()
    wavefront(front(0))
    for layer in range(layers):
        out_share(layer)
        for unit in range(blocks // UNIT):
            spread_end(layer, unit)
        wavefront(rest(layer) + (front(layer + 1) if layer + 1 < layers else []))
    out_ref[...] = stream[...]
    drain()


def local(
    tokens,
    norm_before,
    query_weight,
    key_weight,
    value_weight,
    output_weight,
    norm_after,
    gate_weight,
    up_weight,
    down_weight,
    block_image,
    image_width,
):
    rows = tokens.shape[0]
    blocks = rows // BLK
    layers = query_weight.shape[0]
    place = lax.axis_index(("row", "col"))
    first, width, filled = [
        lax.dynamic_slice_in_dim(table, place * blocks, blocks)
        for table in block_tables(block_image, image_width)
    ]
    cosine, sine = rope_tables(first, width, place * blocks, blocks)
    origin = (place // 8 - 1) * 8 * blocks
    begin = jnp.minimum(first, place * blocks + 8 * blocks - WINDOW)
    window = jnp.stack([begin - origin, (begin - first) * BLK, filled], axis=1)
    hbm = pl.BlockSpec(memory_space=pl.ANY)
    vmem = pl.BlockSpec(memory_space=pltpu.VMEM)
    bf16, f32 = jnp.bfloat16, jnp.float32
    return pl.pallas_call(
        functools.partial(layers_kernel, layers),
        out_shape=jax.ShapeDtypeStruct(tokens.shape, f32),
        in_specs=[pl.BlockSpec(memory_space=pltpu.SMEM)] + [vmem] * 5 + [hbm] * 7,
        out_specs=vmem,
        scratch_shapes=[
            pltpu.VMEM(query_weight.shape, bf16),
            pltpu.VMEM(key_weight.shape, bf16),
            pltpu.VMEM(value_weight.shape, bf16),
            pltpu.VMEM((layers, 8 * BLK, 8 * BLK), bf16),
            pltpu.VMEM(gate_weight.shape, bf16),
            pltpu.VMEM(up_weight.shape, bf16),
            pltpu.VMEM(down_weight.shape, bf16),
            pltpu.VMEM((layers, 8, rows, BLK), bf16),
            pltpu.VMEM((layers, 8, rows, BLK), bf16),
            pltpu.VMEM((24 * blocks, BLK, 2 * BLK), bf16),
            pltpu.VMEM((24 * blocks, BLK, 2 * BLK), bf16),
            pltpu.VMEM((rows, BLK), bf16),
            pltpu.VMEM((2 * BLK, WINDOW * BLK), f32),
            pltpu.VMEM((8, BLK, BLK), f32),
            pltpu.VMEM((layers, 8, rows, BLK), bf16),
            pltpu.VMEM((layers, 3, 2, rows, BLK), bf16),
            pltpu.VMEM((layers, rows, BLK), bf16),
            pltpu.VMEM((layers, rows, BLK), bf16),
            pltpu.VMEM((rows, BLK), f32),
            pltpu.SemaphoreType.DMA((layers + 6,)),
            pltpu.SemaphoreType.DMA((layers, SEMS)),
            pltpu.SemaphoreType.DMA((layers, SEMS)),
        ],
        compiler_params=pltpu.CompilerParams(
            collective_id=0, has_side_effects=True, vmem_limit_bytes=56 << 20
        ),
        name="encoder_layers",
    )(
        window,
        tokens,
        cosine,
        sine,
        norm_before[:, None, :],
        norm_after[:, None, :],
        query_weight,
        key_weight,
        value_weight,
        output_weight,
        gate_weight,
        up_weight,
        down_weight,
    )


def solution(mesh):
    placed = (
        P(("row", "col"), "tp"),
        P(),
        P(None, None, "tp"),
        P(None, None, "tp"),
        P(None, None, "tp"),
        P(None, "tp", None),
        P(),
        P(None, None, "tp"),
        P(None, None, "tp"),
        P(None, "tp", None),
        P(),
        P(),
    )
    return jax.shard_map(
        local, mesh=mesh, in_specs=placed, out_specs=P(("row", "col"), "tp"), check_vma=False
    )
```

time: 252 us -> 189 us (0.75); the launches traced: 249 us -> 189 us
  Pallas kernels: 239 us -> 179 us
    pallas_call x1, Pallas kernels: 239 us -> 179 us  [local(): pl.pallas_call(functools.partial(layers_kernel, layers), out_shape=jax.Sh...]
where the time goes in v2:
time: 189 us
  Pallas kernels  179 us (95%)
  other arithmetic  6.42 us (3%)
  local copies, waits for them, and re-layouts  3.76 us (2%)
    pallas_call x1, Pallas kernels, local(): pl.pallas_call(functools.partial(layers_kernel, layers), out_shape=jax.Sh...  179 us

profile of v2, /device:TPU:4, one launch (start us, length us, event | category | flops | bytes accessed | tf_op | source)
XLA Modules:
  0.0 188.9 jit_solution(4766228089903342651)
XLA Ops:
  0.0 0.8 convert_reduce_fusion
  0.8 0.8 fusion.17
  1.6 0.9 select_reduce_fusion
  2.5 0.7 select_reduce_fusion.2
  3.2 0.1 subtract_multiply_fusion
  3.3 0.1 dynamic_slice.11
  3.3 0.2 fusion.12
  3.6 0.1 slice.6
  3.7 0.1 slice.7
  3.8 0.1 broadcast_multiply_fusion
  3.9 0.2 fusion
  4.1 0.1 copy.42
  4.3 1.0 pad_maximum_fusion.1.sine_ref
  5.2 0.1 copy.38
  5.4 1.0 pad_maximum_fusion.cosine_ref
  6.3 0.1 copy.35
  6.4 0.1 copy.36
  6.5 0.1 dynamic-slice_bitcast_fusion
  6.6 0.1 copy.37
  6.7 0.7 pad_add_fusion.window_ref
  7.4 0.6 copy.45.gain_before_ref
  8.0 0.6 copy.46.gain_after_ref
  8.6 178.7 %encoder_layers.1 = f32[512,128]{1,0:T(8,128)} custom-call(s32[4,3]{1,0:T(4,128)} %pad_add_fusion.window_ref, bf16[512,128]{1,0:T(8,128)(2,1)} %tokens_ref.1, f32[512,128]{1,0:T(8,128)} %pad_maximum_fusion.cosine_ref, f32[512,128]{1,0:T(8,128)} %pad_maximum_fusion.1.sine_ref, bf16[2,1,1024]{2,1,0:T(2,128)(2,1)} %copy.45.gain_before_ref, ...), custom_call_target="tpu_custom_call" | custom-call | tf_op jit(solution)/shard_map/encoder_layers/pallas_call | solution.py:551
  187.2 1.7 copy.48
  (6 shorter events, 0.0 us)
Async XLA Ops:
  0.0 7.4 %copy-start = (bf16[2,1024]{1,0:T(2,128)(2,1)S(1)}, bf16[2,1024]{1,0:T(2,128)(2,1)}, u32[]{:S(2)}) copy-start(bf16[2,1024]{1,0:T(2,128)(2,1)} %param.13) | copy-start | bytes 12292
  0.0 8.0 %copy-start.1 = (bf16[2,1024]{1,0:T(2,128)(2,1)S(1)}, bf16[2,1024]{1,0:T(2,128)(2,1)}, u32[]{:S(2)}) copy-start(bf16[2,1024]{1,0:T(2,128)(2,1)} %param.18) | copy-start | bytes 12292

commit v3 on v2

--- a/solution.py
+++ b/solution.py
@@ -2,6 +2,7 @@
 
 import jax
 import jax.numpy as jnp
+import numpy as np
 from jax import lax
 from jax.experimental import pallas as pl
 from jax.experimental.pallas import tpu as pltpu
@@ -24,40 +25,10 @@
 SEMS = KV + 2 * KV_SEMS
 
 
-def block_tables(block_image, image_width):
-    block_total = block_image.shape[0]
-    images = jnp.arange(image_width.shape[0], dtype=jnp.int32)
-    member = (block_image[:, None] == images[None, :]).astype(jnp.int32)
-    count = jnp.sum(member, axis=0)
-    start = jnp.sum((block_image[:, None] < images[None, :]).astype(jnp.int32), axis=0)
-    slots = count * BLK
-    filled = slots // image_width * image_width
-    first = jnp.sum(member * start[None, :], axis=1)
-    return (
-        first,
-        jnp.sum(member * image_width[None, :], axis=1),
-        jnp.sum(member * filled[None, :], axis=1),
-    )
-
-
-def rope_tables(first, width, first_block, shard_blocks):
+def frequencies():
     half = HEAD_DIM // 2
-    offset = (first_block + jnp.arange(shard_blocks, dtype=jnp.int32) - first) * BLK
-    slot = jnp.repeat(offset, BLK) + jnp.arange(shard_blocks * BLK, dtype=jnp.int32) % BLK
-    width = jnp.repeat(width, BLK)
-    frequency = theta ** (-2.0 * jnp.arange(half, dtype=jnp.float32) / HEAD_DIM)
-    angle = jnp.concatenate(
-        [
-            (slot // width).astype(jnp.float32)[:, None] * frequency[None, 0::2],
-            (slot % width).astype(jnp.float32)[:, None] * frequency[None, 1::2],
-        ],
-        axis=1,
-    )
-    cosine, sine = jnp.cos(angle), jnp.sin(angle)
-    return (
-        jnp.concatenate([cosine] * 4, axis=1),
-        jnp.concatenate([-sine, sine, -sine, sine], axis=1),
-    )
+    each = theta ** (-2.0 * np.arange(half, dtype=np.float64) / HEAD_DIM)
+    return np.tile(np.concatenate([each[0::2], each[1::2]]), 4)[None, :].astype(np.float32)
 
 
 def normalize(values, gain):
@@ -77,12 +48,47 @@
     return heads * cosine + other * sine
 
 
+def tables_kernel(image_ref, width_ref, frequency_ref, window_ref, cosines, sines):
+    blocks = window_ref.shape[0]
+    row, col = lax.axis_index("row"), lax.axis_index("col")
+    first_block = (row * 4 + col) * blocks
+    own_images = [image_ref[first_block + block] for block in range(blocks)]
+
+    def tally(i, found):
+        image = image_ref[i]
+        return tuple(n + jnp.where(image == own, 1, 0) for n, own in zip(found, own_images)) + tuple(
+            n + jnp.where(image < own, 1, 0) for n, own in zip(found[blocks:], own_images)
+        )
+
+    found = lax.fori_loop(0, image_ref.shape[0], tally, (jnp.int32(0),) * (2 * blocks), unroll=8)
+    lane = lax.broadcasted_iota(jnp.int32, (BLK, BLK), 1)
+    by_row = lax.rem(lane, HEAD_DIM // 2) < HEAD_DIM // 4
+    for block in range(blocks):
+        count, first = found[block], found[blocks + block]
+        width = width_ref[own_images[block]]
+        begin = jnp.clip(first, first_block - 7 * blocks, first_block + 8 * blocks - WINDOW)
+        window_ref[block, 0] = begin - (row // 2 - 1) * 8 * blocks
+        window_ref[block, 1] = (begin - first) * BLK
+        window_ref[block, 2] = lax.div(count * BLK, width) * width
+        slot = (
+            lax.broadcasted_iota(jnp.int32, (BLK, BLK), 0) + (first_block + block - first) * BLK
+        ).astype(jnp.float32)
+        wide = jnp.full((BLK, BLK), width, jnp.int32).astype(jnp.float32)
+        patch_row = jnp.floor((slot + 0.5) / wide)
+        angle = jnp.where(by_row, patch_row, slot - patch_row * wide) * frequency_ref[...]
+        cosine, sine = jnp.cos(angle), jnp.sin(angle)
+        cosines[block * BLK : (block + 1) * BLK, :] = cosine
+        sines[block * BLK : (block + 1) * BLK, :] = jnp.where(
+            lax.rem(lane, HEAD_DIM) < HEAD_DIM // 2, -sine, sine
+        )
+
+
 def layers_kernel(
     layers,
     window_ref,
     tokens_ref,
-    cosine_ref,
-    sine_ref,
+    cosines,
+    sines,
     gain_before_ref,
     gain_after_ref,
     wq_hbm,
@@ -133,22 +139,31 @@
     z_up = (row, (col + 1) % 4, tp)
     z_down = (row, (col + 3) % 4, tp)
 
-    own_out_rows = pl.ds(pl.multiple_of(tp * BLK, BLK), BLK)
-    weights = [
-        pltpu.make_async_copy(src, dst, weight_sem.at[i])
-        for i, (src, dst) in enumerate(
-            [(wo_hbm.at[i], wo.at[i, own_out_rows]) for i in range(layers)]
-            + [(wq_hbm, wq), (wk_hbm, wk), (wv_hbm, wv), (wg_hbm, wg), (wu_hbm, wu), (wd_hbm, wd)]
-        )
-    ]
-    for copy in weights:
-        copy.start()
-
     barrier = pltpu.get_barrier_semaphore()
     peers = [at_tp(1), at_tp(2), at_tp(3), z_partner, core_partner, x_full, x_part, z_up, z_down]
     for peer in peers:
         pl.semaphore_signal(barrier, inc=1, device_id=peer, device_id_type=MESH)
     pl.semaphore_wait(barrier, len(peers))
+
+    def weight(number, layer, src, dst):
+        return pltpu.make_async_copy(src.at[layer], dst, weight_sem.at[number, layer])
+
+    own_out_rows = pl.ds(pl.multiple_of(tp * BLK, BLK), BLK)
+
+    def weights_in(layer):
+        return [
+            weight(i, layer, src, dst[layer])
+            for i, (src, dst) in enumerate([(wk_hbm, wk), (wv_hbm, wv), (wq_hbm, wq)])
+        ]
+
+    def weights_out(layer):
+        return weight(3, layer, wo_hbm, wo[layer].at[own_out_rows])
+
+    def weights_feed(layer):
+        return [
+            weight(4 + i, layer, src, dst[layer])
+            for i, (src, dst) in enumerate([(wg_hbm, wg), (wu_hbm, wu), (wd_hbm, wd)])
+        ]
 
     pending = []
 
@@ -204,10 +219,10 @@
         return jnp.concatenate([held[i, span(chunk), :] for i in range(8)], axis=1)
 
     def out_half(layer, number):
-        return wo.at[layer, pl.ds(pl.multiple_of(number * BLK + core * (BLK // 2), 64), BLK // 2)]
+        return wo[layer].at[pl.ds(pl.multiple_of(number * BLK + core * (BLK // 2), 64), BLK // 2)]
 
     def out_cross(layer):
-        weights[layer].wait()
+        weights_out(layer).wait()
         go(send(out_half(layer, tp), out_half(layer, tp), layer, OUT_W, z_partner))
 
     def out_own(layer):
@@ -245,29 +260,38 @@
 
     def project(layer, chunk):
         gather_end(inputs.at[layer], layer, AG_X, chunk)
+        if chunk == 0:
+            for copy in weights_in(layer):
+                copy.wait()
         held_kv = (kv_first, kv_second)[layer]
         at = span(chunk)
         normed = normalize(
             whole_rows(inputs.at[layer], chunk).astype(jnp.float32),
-            gain_before_ref[layer].astype(jnp.float32),
-        )
-        cosine, sine = cosine_ref[at, :], sine_ref[at, :]
+            gain_before_ref[...].astype(jnp.float32)[layer : layer + 1],
+        )
+        cosine, sine = cosines[at, :], sines[at, :]
         here = (8 + core * 4 + col) * blocks + chunk
         held_kv[here, :, 0:BLK] = rotate(
-            jnp.dot(normed, wk[layer], preferred_element_type=jnp.float32), cosine, sine
+            jnp.dot(normed, wk[layer][...], preferred_element_type=jnp.float32), cosine, sine
         ).astype(jnp.bfloat16)
         held_kv[here, :, BLK : 2 * BLK] = jnp.dot(
-            normed, wv[layer], preferred_element_type=jnp.float32
+            normed, wv[layer][...], preferred_element_type=jnp.float32
         ).astype(jnp.bfloat16)
         if chunk % UNIT == UNIT - 1:
             spread_own(layer, chunk // UNIT)
         turned = rotate(
-            jnp.dot(normed, wq[layer], preferred_element_type=jnp.float32), cosine, sine
+            jnp.dot(normed, wq[layer][...], preferred_element_type=jnp.float32), cosine, sine
         ).astype(jnp.bfloat16)
         query[at, :] = turned * jnp.bfloat16(HEAD_DIM**-0.5)
         if chunk == blocks - 1:
             out_own(layer)
             out_pass(layer)
+            if layer == 0:
+                for copy in weights_feed(0):
+                    copy.start()
+                for later in range(1, layers):
+                    for copy in weights_in(later) + [weights_out(later)] + weights_feed(later):
+                        copy.start()
 
     def kv_unit(layer, offset, source, unit):
         number = (offset * 8 + core * 4 + source) * blocks + unit * UNIT
@@ -412,20 +436,22 @@
     def feed(layer, chunk):
         if chunk == 0:
             out_end(layer)
+            for copy in weights_feed(layer):
+                copy.wait()
         gather_end(mixes.at[layer], layer, AG_A, chunk)
         at = span(chunk)
         headed = jnp.dot(
-            whole_rows(mixes.at[layer], chunk), wo[layer], preferred_element_type=jnp.float32
+            whole_rows(mixes.at[layer], chunk), wo[layer][...], preferred_element_type=jnp.float32
         )
         for i in range(8):
             head_part[i] = headed[:, i * BLK : (i + 1) * BLK]
         stream[at, :] = stream[at, :] + head_part[tp]
         middle = whole_rows(inputs.at[layer], chunk).astype(jnp.float32) + headed
-        post = normalize(middle, gain_after_ref[layer].astype(jnp.float32))
-        gate = jnp.dot(post, wg[layer], preferred_element_type=jnp.float32)
-        up = jnp.dot(post, wu[layer], preferred_element_type=jnp.float32)
+        post = normalize(middle, gain_after_ref[...].astype(jnp.float32)[layer : layer + 1])
+        gate = jnp.dot(post, wg[layer][...], preferred_element_type=jnp.float32)
+        up = jnp.dot(post, wu[layer][...], preferred_element_type=jnp.float32)
         hidden = (gate / (1.0 + jnp.exp(-gate)) * up).astype(jnp.bfloat16)
-        part = jnp.dot(hidden, wd[layer], preferred_element_type=jnp.float32)
+        part = jnp.dot(hidden, wd[layer][...], preferred_element_type=jnp.float32)
         for i in range(8):
             parts[layer, i, at, :] = part[:, i * BLK : (i + 1) * BLK].astype(jnp.bfloat16)
         for d in (1, 3, 2):
@@ -506,9 +532,9 @@
     stream[...] = tokens_ref[...].astype(jnp.float32)
     for chunk in range(blocks):
         start_layer(0, chunk)
+    for copy in weights_in(0) + [weights_out(0)]:
+        copy.start()
     out_cross(0)
-    for copy in weights[layers:]:
-        copy.wait()
     wavefront(front(0))
     for layer in range(layers):
         out_share(layer)
@@ -536,31 +562,34 @@
     rows = tokens.shape[0]
     blocks = rows // BLK
     layers = query_weight.shape[0]
-    place = lax.axis_index(("row", "col"))
-    first, width, filled = [
-        lax.dynamic_slice_in_dim(table, place * blocks, blocks)
-        for table in block_tables(block_image, image_width)
-    ]
-    cosine, sine = rope_tables(first, width, place * blocks, blocks)
-    origin = (place // 8 - 1) * 8 * blocks
-    begin = jnp.minimum(first, place * blocks + 8 * blocks - WINDOW)
-    window = jnp.stack([begin - origin, (begin - first) * BLK, filled], axis=1)
     hbm = pl.BlockSpec(memory_space=pl.ANY)
     vmem = pl.BlockSpec(memory_space=pltpu.VMEM)
+    smem = pl.BlockSpec(memory_space=pltpu.SMEM)
     bf16, f32 = jnp.bfloat16, jnp.float32
+    window, cosine, sine = pl.pallas_call(
+        tables_kernel,
+        out_shape=(
+            jax.ShapeDtypeStruct((blocks, 3), jnp.int32),
+            jax.ShapeDtypeStruct((rows, BLK), f32),
+            jax.ShapeDtypeStruct((rows, BLK), f32),
+        ),
+        in_specs=[smem, smem, vmem],
+        out_specs=(smem, vmem, vmem),
+        name="tables",
+    )(block_image, image_width, frequencies())
     return pl.pallas_call(
         functools.partial(layers_kernel, layers),
         out_shape=jax.ShapeDtypeStruct(tokens.shape, f32),
-        in_specs=[pl.BlockSpec(memory_space=pltpu.SMEM)] + [vmem] * 5 + [hbm] * 7,
+        in_specs=[smem] + [vmem] * 5 + [hbm] * 7,
         out_specs=vmem,
         scratch_shapes=[
-            pltpu.VMEM(query_weight.shape, bf16),
-            pltpu.VMEM(key_weight.shape, bf16),
-            pltpu.VMEM(value_weight.shape, bf16),
-            pltpu.VMEM((layers, 8 * BLK, 8 * BLK), bf16),
-            pltpu.VMEM(gate_weight.shape, bf16),
-            pltpu.VMEM(up_weight.shape, bf16),
-            pltpu.VMEM(down_weight.shape, bf16),
+            [pltpu.VMEM(query_weight.shape[1:], bf16)] * layers,
+            [pltpu.VMEM(key_weight.shape[1:], bf16)] * layers,
+            [pltpu.VMEM(value_weight.shape[1:], bf16)] * layers,
+            [pltpu.VMEM((8 * BLK, 8 * BLK), bf16)] * layers,
+            [pltpu.VMEM(gate_weight.shape[1:], bf16)] * layers,
+            [pltpu.VMEM(up_weight.shape[1:], bf16)] * layers,
+            [pltpu.VMEM(down_weight.shape[1:], bf16)] * layers,
             pltpu.VMEM((layers, 8, rows, BLK), bf16),
             pltpu.VMEM((layers, 8, rows, BLK), bf16),
             pltpu.VMEM((24 * blocks, BLK, 2 * BLK), bf16),
@@ -573,7 +602,7 @@
             pltpu.VMEM((layers, rows, BLK), bf16),
             pltpu.VMEM((layers, rows, BLK), bf16),
             pltpu.VMEM((rows, BLK), f32),
-            pltpu.SemaphoreType.DMA((layers + 6,)),
+            pltpu.SemaphoreType.DMA((7, layers)),
             pltpu.SemaphoreType.DMA((layers, SEMS)),
             pltpu.SemaphoreType.DMA((layers, SEMS)),
         ],
@@ -586,8 +615,8 @@
         tokens,
         cosine,
         sine,
-        norm_before[:, None, :],
-        norm_after[:, None, :],
+        norm_before,
+        norm_after,
         query_weight,
         key_weight,
         value_weight,

time: 189 us -> 183 us (0.968)
  other arithmetic: 6.42 us -> 0 us
  local copies, waits for them, and re-layouts: 3.76 us -> 1.67 us
  Pallas kernels: 179 us -> 181 us
    pallas_call x0 -> x1, Pallas kernels: none -> 3.78 us  [local(): pl.pallas_call(tables_kernel, out_shape=(jax.ShapeDtypeStruct((blocks, 3)...]
    reduce_sum x3 -> x0, other arithmetic: 2.4 us -> none  [the longest x1 0.87 us: block_tables(): jnp.sum(member * image_width[None, :], axis=1)]
    concatenate x2 -> x0, other arithmetic: 1.95 us -> none  [the longest x1 0.98 us: rope_tables(): jnp.concatenate([cosine] * 4, axis=1)]
where the time goes in v3:
time: 183 us
  Pallas kernels  181 us (99%)
    pallas_call x1, Pallas kernels, local(): pl.pallas_call(functools.partial(layers_kernel, layers), out_shape=jax.Sh...  177 us
    pallas_call x1, Pallas kernels, local(): pl.pallas_call(tables_kernel, out_shape=(jax.ShapeDtypeStruct((blocks, 3)...  3.78 us

profile of v3, /device:TPU:4, one launch (start us, length us, event | category | flops | bytes accessed | tf_op | source)
XLA Modules:
  0.0 182.6 jit_solution(8906446563065827407)
XLA Ops:
  0.0 3.8 %tables.1 = (s32[4,3]{1,0:T(4,128)}, f32[512,128]{1,0:T(8,128)}, f32[512,128]{1,0:T(8,128)}) custom-call(s32[128]{0:T(128)} %image_ref.1, s32[8]{0:T(128)} %width_ref.1, f32[1,128]{1,0:T(1,128)} %constant.2.clone.frequency_ref), custom_call_target="tpu_custom_call" | custom-call | tf_op jit(solution)/shard_map/tables/pallas_call | solution.py:569
  3.8 177.1 %encoder_layers.1 = f32[512,128]{1,0:T(8,128)} custom-call(s32[4,3]{1,0:T(4,128)} %get-tuple-element.8.window_ref, bf16[512,128]{1,0:T(8,128)(2,1)} %tokens_ref.1, f32[512,128]{1,0:T(8,128)} %get-tuple-element.9.cosines, f32[512,128]{1,0:T(8,128)} %get-tuple-element.10.sines, bf16[2,1024]{1,0:T(2,128)(2,1)} %gain_before_ref.1, ...), custom_call_target="tpu_custom_call" | custom-call | tf_op jit(solution)/shard_map/encoder_layers/pallas_call | solution.py:580
  180.9 1.7 copy.15

commit v4 on v3

--- a/solution.py
+++ b/solution.py
@@ -18,6 +18,7 @@
 masked = -1e30
 MESH = pl.DeviceIdType.MESH
 
+LAG = 3
 UNIT = 2
 
 AG_X, AG_A, RS_Y, OUT_W, KV = 0, 32, 64, 80, 96
@@ -48,23 +49,19 @@
     return heads * cosine + other * sine
 
 
-def tables_kernel(image_ref, width_ref, frequency_ref, window_ref, cosines, sines):
+def tables_kernel(image_ref, images_ref, width_ref, frequency_ref, window_ref, cosines, sines):
     blocks = window_ref.shape[0]
     row, col = lax.axis_index("row"), lax.axis_index("col")
     first_block = (row * 4 + col) * blocks
     own_images = [image_ref[first_block + block] for block in range(blocks)]
 
-    def tally(i, found):
-        image = image_ref[i]
-        return tuple(n + jnp.where(image == own, 1, 0) for n, own in zip(found, own_images)) + tuple(
-            n + jnp.where(image < own, 1, 0) for n, own in zip(found[blocks:], own_images)
-        )
-
-    found = lax.fori_loop(0, image_ref.shape[0], tally, (jnp.int32(0),) * (2 * blocks), unroll=8)
+    images = images_ref[...]
     lane = lax.broadcasted_iota(jnp.int32, (BLK, BLK), 1)
     by_row = lax.rem(lane, HEAD_DIM // 2) < HEAD_DIM // 4
     for block in range(blocks):
-        count, first = found[block], found[blocks + block]
+        own = own_images[block]
+        count = jnp.sum(jnp.where(images == own, 1, 0))
+        first = jnp.sum(jnp.where(images < own, 1, 0))
         width = width_ref[own_images[block]]
         begin = jnp.clip(first, first_block - 7 * blocks, first_block + 8 * blocks - WINDOW)
         window_ref[block, 0] = begin - (row // 2 - 1) * 8 * blocks
@@ -139,31 +136,34 @@
     z_up = (row, (col + 1) % 4, tp)
     z_down = (row, (col + 3) % 4, tp)
 
+    def weight(number, layer, src, dst):
+        return pltpu.make_async_copy(src.at[layer], dst, weight_sem.at[number, layer])
+
+    own_out_rows = pl.ds(pl.multiple_of(tp * BLK, BLK), BLK)
+
+    def weights_in(layer):
+        return [
+            weight(i, layer, src, dst[layer])
+            for i, (src, dst) in enumerate([(wk_hbm, wk), (wv_hbm, wv), (wq_hbm, wq)])
+        ]
+
+    def weights_out(layer):
+        return weight(3, layer, wo_hbm, wo[layer].at[own_out_rows])
+
+    def weights_feed(layer):
+        return [
+            weight(4 + i, layer, src, dst[layer])
+            for i, (src, dst) in enumerate([(wg_hbm, wg), (wu_hbm, wu), (wd_hbm, wd)])
+        ]
+
+    for copy in weights_in(0) + [weights_out(0)]:
+        copy.start()
+
     barrier = pltpu.get_barrier_semaphore()
     peers = [at_tp(1), at_tp(2), at_tp(3), z_partner, core_partner, x_full, x_part, z_up, z_down]
     for peer in peers:
         pl.semaphore_signal(barrier, inc=1, device_id=peer, device_id_type=MESH)
     pl.semaphore_wait(barrier, len(peers))
-
-    def weight(number, layer, src, dst):
-        return pltpu.make_async_copy(src.at[layer], dst, weight_sem.at[number, layer])
-
-    own_out_rows = pl.ds(pl.multiple_of(tp * BLK, BLK), BLK)
-
-    def weights_in(layer):
-        return [
-            weight(i, layer, src, dst[layer])
-            for i, (src, dst) in enumerate([(wk_hbm, wk), (wv_hbm, wv), (wq_hbm, wq)])
-        ]
-
-    def weights_out(layer):
-        return weight(3, layer, wo_hbm, wo[layer].at[own_out_rows])
-
-    def weights_feed(layer):
-        return [
-            weight(4 + i, layer, src, dst[layer])
-            for i, (src, dst) in enumerate([(wg_hbm, wg), (wu_hbm, wu), (wd_hbm, wd)])
-        ]
 
     pending = []
 
@@ -259,6 +259,8 @@
         gather_pass(inputs.at[layer], layer, AG_X, chunk)
 
     def project(layer, chunk):
+        if layer == 0 and chunk == 0:
+            out_cross(0)
         gather_end(inputs.at[layer], layer, AG_X, chunk)
         if chunk == 0:
             for copy in weights_in(layer):
@@ -507,11 +509,11 @@
         return run
 
     def wavefront(stages):
-        for step in range(blocks + len(stages) - 1):
+        for step in range(blocks + LAG * (len(stages) - 1)):
             for i in reversed(range(len(stages))):
-                if 0 <= step - i < blocks:
+                if 0 <= step - LAG * i < blocks:
                     layer, stage = stages[i]
-                    stage(layer, step - i)
+                    stage(layer, step - LAG * i)
 
     def chain(step):
         return in_units(lambda layer, unit: spread_next(layer, unit, step))
@@ -532,9 +534,6 @@
     stream[...] = tokens_ref[...].astype(jnp.float32)
     for chunk in range(blocks):
         start_layer(0, chunk)
-    for copy in weights_in(0) + [weights_out(0)]:
-        copy.start()
-    out_cross(0)
     wavefront(front(0))
     for layer in range(layers):
         out_share(layer)
@@ -573,10 +572,10 @@
             jax.ShapeDtypeStruct((rows, BLK), f32),
             jax.ShapeDtypeStruct((rows, BLK), f32),
         ),
-        in_specs=[smem, smem, vmem],
+        in_specs=[smem, vmem, smem, vmem],
         out_specs=(smem, vmem, vmem),
         name="tables",
-    )(block_image, image_width, frequencies())
+    )(block_image, block_image[None, :], image_width, frequencies())
     return pl.pallas_call(
         functools.partial(layers_kernel, layers),
         out_shape=jax.ShapeDtypeStruct(tokens.shape, f32),

time: 183 us -> 153 us (0.84)
  Pallas kernels: 181 us -> 150 us
    pallas_call x1, Pallas kernels: 177 us -> 148 us  [local(): pl.pallas_call(functools.partial(layers_kernel, layers), out_shape=jax.Sh...]
where the time goes in v4:
time: 153 us; the launch traced here: 152 us
  Pallas kernels  150 us (98%)
  local copies, waits for them, and re-layouts  1.67 us (1%)
    pallas_call x1, Pallas kernels, local(): pl.pallas_call(functools.partial(layers_kernel, layers), out_shape=jax.Sh...  148 us

profile of v4, /device:TPU:4, one launch (start us, length us, event | category | flops | bytes accessed | tf_op | source)
XLA Modules:
  0.0 152.2 jit_solution(11903238570439781479)
XLA Ops:
  0.0 2.8 %tables.1 = (s32[4,3]{1,0:T(4,128)}, f32[512,128]{1,0:T(8,128)}, f32[512,128]{1,0:T(8,128)}) custom-call(s32[128]{0:T(128)} %image_ref.1, s32[1,128]{1,0:T(1,128)} %bitcast.1, s32[8]{0:T(128)} %width_ref.1, f32[1,128]{1,0:T(1,128)} %constant.2.clone.frequency_ref), custom_call_target="tpu_custom_call" | custom-call | tf_op jit(solution)/shard_map/tables/pallas_call | solution.py:568
  2.8 147.7 %encoder_layers.1 = f32[512,128]{1,0:T(8,128)} custom-call(s32[4,3]{1,0:T(4,128)} %get-tuple-element.8.window_ref, bf16[512,128]{1,0:T(8,128)(2,1)} %tokens_ref.1, f32[512,128]{1,0:T(8,128)} %get-tuple-element.9.cosines, f32[512,128]{1,0:T(8,128)} %get-tuple-element.10.sines, bf16[2,1024]{1,0:T(2,128)(2,1)} %gain_before_ref.1, ...), custom_call_target="tpu_custom_call" | custom-call | tf_op jit(solution)/shard_map/encoder_layers/pallas_call | solution.py:579
  150.5 1.7 %copy.15 = f32[512,128]{1,0:T(8,128)} copy(f32[512,128]{1,0:T(8,128)} %encoder_layers.1) | data formatting | bytes 524288

commit v5 on v4

--- a/solution.py
+++ b/solution.py
@@ -18,12 +18,12 @@
 masked = -1e30
 MESH = pl.DeviceIdType.MESH
 
-LAG = 3
+FAR, NEAR, HOP = 3, 3, 3
 UNIT = 2
 
 AG_X, AG_A, RS_Y, OUT_W, KV = 0, 32, 64, 80, 96
 KV_UP, KV_DOWN, KV_FULL, KV_PART, KV_CORE, KV_BACK, KV_SEMS = 0, 4, 8, 12, 16, 20, 24
-SEMS = KV + 2 * KV_SEMS
+SEMS = KV + 4 // UNIT * KV_SEMS
 
 
 def frequencies():
@@ -115,6 +115,7 @@
     half_out,
     half_in,
     stream,
+    stream_other,
     weight_sem,
     send_sem,
     recv_sem,
@@ -181,8 +182,11 @@
         copy.start()
         pending.append((None, copy))
 
-    def drain():
-        for needed, copy in pending:
+    marks = {}
+
+    def drain(mark=None):
+        done = pending[: marks[mark] if mark else len(pending)]
+        for needed, copy in done:
             if needed is None:
                 copy.wait_send()
             else:
@@ -191,7 +195,7 @@
                 def _(copy=copy):
                     copy.wait_send()
 
-        pending.clear()
+        del pending[: len(done)]
 
     def span(chunk):
         return pl.ds(chunk * BLK, BLK)
@@ -252,15 +256,23 @@
             send(held, held, layer, OUT_W + 8 + i, core_partner).wait_recv()
 
     def start_layer(layer, chunk):
-        inputs[layer, tp, span(chunk), :] = stream[span(chunk), :].astype(jnp.bfloat16)
-        gather_own(inputs.at[layer], layer, AG_X, chunk)
+        held = inputs.at[layer]
+        held[tp, span(chunk), :] = stream[span(chunk), :].astype(jnp.bfloat16)
+        if layer == 0:
+            gather_own(held, layer, AG_X, chunk)
+        else:
+            held[other, span(chunk), :] = stream_other[span(chunk), :].astype(jnp.bfloat16)
+            for slot, sem in ((tp, 0), (other, 3)):
+                piece = held.at[slot, span(chunk)]
+                for d in (1, 3, 2):
+                    go(send(piece, piece, layer, AG_X + 8 * chunk + sem + d, at_tp(d)))
 
     def pass_layer(layer, chunk):
         gather_pass(inputs.at[layer], layer, AG_X, chunk)
 
     def project(layer, chunk):
-        if layer == 0 and chunk == 0:
-            out_cross(0)
+        if layer > 0 and chunk == 0:
+            marks["layer"] = len(pending)
         gather_end(inputs.at[layer], layer, AG_X, chunk)
         if chunk == 0:
             for copy in weights_in(layer):
@@ -391,6 +403,8 @@
                 [held_kv[begin + chunk * each + i][:, lanes : lanes + BLK] for i in range(each)], axis=0
             )
 
+        if layer + 1 == layers and block == 0:
+            marks["attend"] = len(pending)
         at = span(block)
         begin = window_ref[block, 0]
         shift = window_ref[block, 1]
@@ -437,6 +451,8 @@
 
     def feed(layer, chunk):
         if chunk == 0:
+            if layer + 1 == layers:
+                drain("attend")
             out_end(layer)
             for copy in weights_feed(layer):
                 copy.wait()
@@ -448,6 +464,9 @@
         for i in range(8):
             head_part[i] = headed[:, i * BLK : (i + 1) * BLK]
         stream[at, :] = stream[at, :] + head_part[tp]
+        if layer + 1 < layers:
+            before = inputs[layer, other, at, :].astype(jnp.float32) if layer == 0 else stream_other[at, :]
+            stream_other[at, :] = before + head_part[other]
         middle = whole_rows(inputs.at[layer], chunk).astype(jnp.float32) + headed
         post = normalize(middle, gain_after_ref[...].astype(jnp.float32)[layer : layer + 1])
         gate = jnp.dot(post, wg[layer][...], preferred_element_type=jnp.float32)
@@ -471,9 +490,10 @@
         )
 
     def cross_send(layer, chunk):
+        halves = pl.ds(0, 2 if layer + 1 < layers else 1)
         return send(
-            half_out.at[layer, span(chunk)],
-            half_in.at[layer, span(chunk)],
+            half_out.at[layer, halves, span(chunk)],
+            half_in.at[layer, halves, span(chunk)],
             layer,
             RS_Y + 4 * chunk,
             z_partner,
@@ -490,15 +510,21 @@
                 total = total + parts_in[layer, d, half, at, :].astype(jnp.float32)
             return total
 
-        half_out[layer, at, :] = summed(1 - low).astype(jnp.bfloat16)
+        theirs, own = summed(1 - low), summed(low)
+        half_out[layer, 0, at, :] = theirs.astype(jnp.bfloat16)
+        if layer + 1 < layers:
+            half_out[layer, 1, at, :] = own.astype(jnp.bfloat16)
         go(cross_send(layer, chunk))
-        stream[at, :] = stream[at, :] + summed(low)
+        stream[at, :] = stream[at, :] + own
+        if layer + 1 < layers:
+            stream_other[at, :] = stream_other[at, :] + theirs
 
     def finish(layer, chunk):
         at = span(chunk)
         cross_send(layer, chunk).wait_recv()
-        stream[at, :] = stream[at, :] + half_in[layer, at, :].astype(jnp.float32)
+        stream[at, :] = stream[at, :] + half_in[layer, 0, at, :].astype(jnp.float32)
         if layer + 1 < layers:
+            stream_other[at, :] = stream_other[at, :] + half_in[layer, 1, at, :].astype(jnp.float32)
             start_layer(layer + 1, chunk)
 
     def in_units(stage):
@@ -509,33 +535,44 @@
         return run
 
     def wavefront(stages):
-        for step in range(blocks + LAG * (len(stages) - 1)):
-            for i in reversed(range(len(stages))):
-                if 0 <= step - LAG * i < blocks:
-                    layer, stage = stages[i]
-                    stage(layer, step - LAG * i)
+        first, offsets = 0, []
+        for _, _, lag in stages:
+            first += lag if offsets else 0
+            offsets.append(first)
+        for step in range(blocks + first):
+            for (layer, stage, _), offset in reversed(list(zip(stages, offsets))):
+                if 0 <= step - offset < blocks:
+                    stage(layer, step - offset)
 
     def chain(step):
         return in_units(lambda layer, unit: spread_next(layer, unit, step))
 
     def front(layer):
+        return ([(layer, pass_layer, FAR)] if layer == 0 else []) + [
+            (layer, project, NEAR),
+            (layer, chain(1), HOP),
+            (layer, chain(2), HOP),
+            (layer, chain(3), HOP),
+            (layer, in_units(spread_back), HOP),
+        ]
+
+    def rest(layer):
         return [
-            (layer, pass_layer),
-            (layer, project),
-            (layer, chain(1)),
-            (layer, chain(2)),
-            (layer, chain(3)),
-            (layer, in_units(spread_back)),
+            (layer, attend, 0),
+            (layer, pass_mix, FAR),
+            (layer, feed, NEAR),
+            (layer, add_up, NEAR),
+            (layer, finish, FAR),
         ]
-
-    def rest(layer):
-        return [(layer, attend), (layer, pass_mix), (layer, feed), (layer, add_up), (layer, finish)]
 
     stream[...] = tokens_ref[...].astype(jnp.float32)
     for chunk in range(blocks):
         start_layer(0, chunk)
+    out_cross(0)
     wavefront(front(0))
     for layer in range(layers):
+        if layer > 0:
+            drain("layer")
         out_share(layer)
         for unit in range(blocks // UNIT):
             spread_end(layer, unit)
@@ -598,8 +635,9 @@
             pltpu.VMEM((8, BLK, BLK), f32),
             pltpu.VMEM((layers, 8, rows, BLK), bf16),
             pltpu.VMEM((layers, 3, 2, rows, BLK), bf16),
-            pltpu.VMEM((layers, rows, BLK), bf16),
-            pltpu.VMEM((layers, rows, BLK), bf16),
+            pltpu.VMEM((layers, 2, rows, BLK), bf16),
+            pltpu.VMEM((layers, 2, rows, BLK), bf16),
+            pltpu.VMEM((rows, BLK), f32),
             pltpu.VMEM((rows, BLK), f32),
             pltpu.SemaphoreType.DMA((7, layers)),
             pltpu.SemaphoreType.DMA((layers, SEMS)),

time: 153 us -> 151 us (0.987)
    pallas_call x1, Pallas kernels: 148 us -> 146 us  [local(): pl.pallas_call(functools.partial(layers_kernel, layers), out_shape=jax.Sh...]
where the time goes in v5:
time: 151 us; the launch traced here: 150 us
  Pallas kernels  149 us (99%)
  local copies, waits for them, and re-layouts  1.67 us (1%)
    pallas_call x1, Pallas kernels, local(): pl.pallas_call(functools.partial(layers_kernel, layers), out_shape=jax.Sh...  146 us

profile of v5, /device:TPU:4, one launch (start us, length us, event | category | flops | bytes accessed | tf_op | source)
XLA Modules:
  0.0 150.2 jit_solution(4712291081175184219)
XLA Ops:
  0.0 2.8 %tables.1 = (s32[4,3]{1,0:T(4,128)}, f32[512,128]{1,0:T(8,128)}, f32[512,128]{1,0:T(8,128)}) custom-call(s32[128]{0:T(128)} %image_ref.1, s32[1,128]{1,0:T(1,128)} %bitcast.1, s32[8]{0:T(128)} %width_ref.1, f32[1,128]{1,0:T(1,128)} %constant.2.clone.frequency_ref), custom_call_target="tpu_custom_call" | custom-call | tf_op jit(solution)/shard_map/tables/pallas_call | solution.py:605
  2.8 145.8 %encoder_layers.1 = f32[512,128]{1,0:T(8,128)} custom-call(s32[4,3]{1,0:T(4,128)} %get-tuple-element.8.window_ref, bf16[512,128]{1,0:T(8,128)(2,1)} %tokens_ref.1, f32[512,128]{1,0:T(8,128)} %get-tuple-element.9.cosines, f32[512,128]{1,0:T(8,128)} %get-tuple-element.10.sines, bf16[2,1024]{1,0:T(2,128)(2,1)} %gain_before_ref.1, ...), custom_call_target="tpu_custom_call" | custom-call | tf_op jit(solution)/shard_map/encoder_layers/pallas_call | solution.py:616
  148.6 1.7 %copy.15 = f32[512,128]{1,0:T(8,128)} copy(f32[512,128]{1,0:T(8,128)} %encoder_layers.1) | data formatting | bytes 524288

commit v6 on v5

--- a/solution.py
+++ b/solution.py
@@ -19,7 +19,7 @@
 MESH = pl.DeviceIdType.MESH
 
 FAR, NEAR, HOP = 3, 3, 3
-UNIT = 2
+UNIT = 1
 
 AG_X, AG_A, RS_Y, OUT_W, KV = 0, 32, 64, 80, 96
 KV_UP, KV_DOWN, KV_FULL, KV_PART, KV_CORE, KV_BACK, KV_SEMS = 0, 4, 8, 12, 16, 20, 24

time: 151 us -> 149 us (0.987)
  Pallas kernels: 149 us -> 146 us
    pallas_call x1, Pallas kernels: 146 us -> 143 us  [local(): pl.pallas_call(functools.partial(layers_kernel, layers), out_shape=jax.Sh...]
where the time goes in v6:
time: 149 us; the launch traced here: 148 us
  Pallas kernels  146 us (98%)
  local copies, waits for them, and re-layouts  1.67 us (1%)
    pallas_call x1, Pallas kernels, local(): pl.pallas_call(functools.partial(layers_kernel, layers), out_shape=jax.Sh...  143 us

profile of v6, /device:TPU:4, one launch (start us, length us, event | category | flops | bytes accessed | tf_op | source)
XLA Modules:
  0.0 147.8 jit_solution(17121187196490295785)
XLA Ops:
  0.0 2.8 %tables.1 = (s32[4,3]{1,0:T(4,128)}, f32[512,128]{1,0:T(8,128)}, f32[512,128]{1,0:T(8,128)}) custom-call(s32[128]{0:T(128)} %image_ref.1, s32[1,128]{1,0:T(1,128)} %bitcast.1, s32[8]{0:T(128)} %width_ref.1, f32[1,128]{1,0:T(1,128)} %constant.2.clone.frequency_ref), custom_call_target="tpu_custom_call" | custom-call | tf_op jit(solution)/shard_map/tables/pallas_call | solution.py:605
  2.8 143.4 %encoder_layers.1 = f32[512,128]{1,0:T(8,128)} custom-call(s32[4,3]{1,0:T(4,128)} %get-tuple-element.8.window_ref, bf16[512,128]{1,0:T(8,128)(2,1)} %tokens_ref.1, f32[512,128]{1,0:T(8,128)} %get-tuple-element.9.cosines, f32[512,128]{1,0:T(8,128)} %get-tuple-element.10.sines, bf16[2,1024]{1,0:T(2,128)(2,1)} %gain_before_ref.1, ...), custom_call_target="tpu_custom_call" | custom-call | tf_op jit(solution)/shard_map/encoder_layers/pallas_call | solution.py:616
  146.2 1.7 %copy.15 = f32[512,128]{1,0:T(8,128)} copy(f32[512,128]{1,0:T(8,128)} %encoder_layers.1) | data formatting | bytes 524288
